TPU v7x, 32 devices: a whole 2x2x4 slice. The times are simulated.
32 devices in a mesh: dp: 16 (over z, y, core), tensor: 2 (over x).
Axes of the slice: x: 2, y: 2, z: 4, core: 2. Of those that a mesh axis runs over, the one named last changes fastest.
Arguments:
- layer_in: bfloat16 [262144, 1024], P('dp', 'tensor'), may hold values from -6 to 6
- out_grad: bfloat16 [262144, 1024], P('dp', 'tensor'), may hold values from -6 to 6
- route_index: int32 [128, 256], P('dp'), may hold values from 0 to 2047, as said below
- segments: int32 [262144], P('dp'), may hold values from 0 to 511, never falling along the last dimension, each value on 1 to 2048 neighbouring positions
- w_project: bfloat16 [3, 1024, 1024], P(None, None, 'tensor'), may hold values from -0.1875 to 0.1875
- w_output: bfloat16 [1024, 1024], P('tensor'), may hold values from -0.75 to 0.75
- w_expand: bfloat16 [1024, 4096], P(None, 'tensor'), may hold values from -0.1875 to 0.1875
- w_reduce: bfloat16 [4096, 1024], P('tensor'), may hold values from -0.125 to 0.125
- gain_first: bfloat16 [1024], replicated, may hold values from 0.5 to 1.5
- gain_second: bfloat16 [1024], replicated, may hold values from 0.5 to 1.5
- w_router: bfloat16 [1024], replicated, may hold values from -0.1875 to 0.1875
Outputs:
- layer_out: bfloat16 [262144, 1024], P('dp', 'tensor')
- input_grad: bfloat16 [262144, 1024], P('dp', 'tensor')
- grad_project: float32 [3, 1024, 1024], P(None, None, 'tensor')
- grad_output: float32 [1024, 1024], P('tensor')
- grad_expand: float32 [1024, 4096], P(None, 'tensor')
- grad_reduce: float32 [4096, 1024], P('tensor')
- grad_gain_first: float32 [1024], P('tensor')
- grad_gain_second: float32 [1024], P('tensor')
- grad_router: float32 [1024], P('tensor')
Inputs may be any that keep to these rules, and one draw needn't show every extreme that they name: `route_index`: each row holds 256 distinct positions of one sequence in increasing order. `segments`: document numbers never fall along the tokens; a document has 1 to 2048 tokens and may run past a sequence's end.
All inputs are finite; a program needn't handle non-finite values.
Results may differ from a plain program's by a relative error of at most 0.012.
The roundings to bfloat16 on the way count: a program that leaves them out, or rounds other values in their place, can miss the bound.
Values may be sent and summed in bfloat16 or wider, within the bound.
No kernel may reach another device: no remote copies, remote signals or barrier semaphores. Data moves between devices by JAX's collectives and lax.ppermute only.
A program may use at most 320 MiB of HBM per device.

v0:
```python
from functools import partial

import jax
import jax.numpy as jnp
from jax import lax
from jax.sharding import PartitionSpec as P

HEAD_DIM = 64


def rms_scale(values_in):
    return lax.rsqrt(jnp.mean(values_in * values_in, axis=-1, keepdims=True) + 1e-06)


def shards(
    layer_in,
    out_grad,
    route_index,
    segments,
    w_project,
    w_output,
    w_expand,
    w_reduce,
    gain_first,
    gain_second,
    w_router,
):
    f32 = jnp.float32
    bf16 = jnp.bfloat16
    seq_local, capacity = route_index.shape
    seq_len = layer_in.shape[0] // seq_local
    width_local = layer_in.shape[1]
    full_width = gain_first.shape[0]
    head_dim = HEAD_DIM
    score_scale = head_dim ** (-0.5)
    routed = seq_local * capacity
    start_col = lax.axis_index("tensor") * width_local
    first_local = lax.dynamic_slice_in_dim(gain_first, start_col, width_local).astype(f32)
    second_local = lax.dynamic_slice_in_dim(gain_second, start_col, width_local).astype(f32)
    router_local = lax.dynamic_slice_in_dim(w_router, start_col, width_local).astype(f32)
    flat_rows = (jnp.arange(seq_local, dtype=jnp.int32)[:, None] * seq_len + route_index).reshape(
        -1
    )
    doc_ids = segments[flat_rows].reshape(seq_local, capacity)
    allowed = (route_index[:, None, :] <= route_index[:, :, None]) & (
        doc_ids[:, None, :] == doc_ids[:, :, None]
    )
    rows_local = layer_in[flat_rows]
    cot_local = out_grad[flat_rows]
    rows_float = rows_local.astype(f32)
    cot_float = cot_local.astype(f32)

    def attend_scores(queries, key_rows):
        scores = (
            jnp.einsum("sqhe,skhe->shqk", queries, key_rows, preferred_element_type=f32)
            * score_scale
        )
        return jnp.where(allowed[:, None], scores, -1e30)

    def forward_rows(rows_full):
        full_float = rows_full.astype(f32)
        scale_first = rms_scale(full_float)
        router = jnp.dot(rows_full, w_router, preferred_element_type=f32)
        normed = (full_float * scale_first * gain_first.astype(f32)).astype(bf16)
        project = jnp.einsum("rd,cde->cre", normed, w_project, preferred_element_type=f32).astype(
            bf16
        )
        shaped = project.reshape(3, seq_local, capacity, -1, head_dim)
        queries = shaped[0]
        key_rows = shaped[1]
        value_rows = shaped[2]
        scores = attend_scores(queries, key_rows)
        row_top = jnp.max(scores, axis=-1, keepdims=True)
        row_expo = jnp.exp(scores - row_top)
        row_total = jnp.sum(row_expo, axis=-1, keepdims=True)
        attend_prob = row_expo / row_total
        log_total = row_top + jnp.log(row_total)
        attended = jnp.einsum(
            "shqk,skhe->sqhe", attend_prob.astype(bf16), value_rows, preferred_element_type=f32
        )
        attended = attended.astype(bf16).reshape(routed, -1)
        attn_part = jnp.dot(attended, w_output, preferred_element_type=f32)
        attn_local = lax.psum_scatter(attn_part, "tensor", scatter_dimension=1, tiled=True)
        hidden_local = rows_float + attn_local
        square_sum = lax.psum(jnp.sum(hidden_local * hidden_local, axis=-1), "tensor")
        scale_second = lax.rsqrt(square_sum / full_width + 1e-06)[:, None]
        normed_local = (hidden_local * scale_second * second_local).astype(bf16)
        normed_two = lax.all_gather(normed_local, "tensor", axis=1, tiled=True)
        expand = jnp.dot(normed_two, w_expand, preferred_element_type=f32)
        activated = jax.nn.gelu(expand, approximate=True).astype(bf16)
        return (
            router,
            scale_first,
            normed,
            queries,
            key_rows,
            value_rows,
            log_total,
            attended,
            attn_part,
            attn_local,
            hidden_local,
            scale_second,
            normed_two,
            expand,
            activated,
        )

    rows_full = lax.all_gather(rows_local, "tensor", axis=1, tiled=True)
    (
        router,
        scale_first,
        normed,
        queries,
        key_rows,
        value_rows,
        log_total,
        attended,
        attn_part,
        attn_local,
        hidden_local,
        scale_second,
        normed_two,
        expand,
        activated,
    ) = forward_rows(rows_full)
    mixer_part = jnp.dot(activated, w_reduce, preferred_element_type=f32)
    mixer_local = lax.psum_scatter(
        mixer_part.astype(jnp.bfloat16), "tensor", scatter_dimension=1, tiled=True
    ).astype(jnp.float32)
    branch_local = attn_local + mixer_local
    layer_rows = rows_float + router[:, None] * branch_local
    layer_out = layer_in.at[flat_rows].set(layer_rows.astype(bf16))
    rows_again, cot_full = (
        lax.all_gather(rows_local, "tensor", axis=1, tiled=True),
        lax.all_gather(cot_local, "tensor", axis=1, tiled=True),
    )
    (
        router,
        scale_first,
        normed,
        queries,
        key_rows,
        value_rows,
        log_total,
        attended,
        attn_part,
        attn_local,
        hidden_local,
        scale_second,
        normed_two,
        expand,
        activated,
    ) = forward_rows(rows_again)
    mixer_again = jnp.dot(activated, w_reduce, preferred_element_type=f32)
    router_part = jnp.sum(cot_full.astype(f32) * (attn_part + mixer_again), axis=-1)
    mixer_grad = (router[:, None] * cot_full.astype(f32)).astype(bf16)
    grad_reduce = jnp.einsum("rf,rd->fd", activated, mixer_grad, preferred_element_type=f32)
    act_grad = jnp.einsum("rd,fd->rf", mixer_grad, w_reduce, preferred_element_type=f32)
    gelu_back = jax.vjp(partial(jax.nn.gelu, approximate=True), expand)[1]
    expand_grad = gelu_back(act_grad)[0].astype(bf16)
    grad_expand = jnp.einsum("rd,rf->df", normed_two, expand_grad, preferred_element_type=f32)
    normed_two_part = jnp.einsum("rf,df->rd", expand_grad, w_expand, preferred_element_type=f32)
    normed_two_grad = lax.psum_scatter(normed_two_part, "tensor", scatter_dimension=1, tiled=True)
    hidden_hat = hidden_local * scale_second
    weighted_two = normed_two_grad * second_local
    grad_gain_second = jnp.sum(normed_two_grad * hidden_hat, axis=0)
    router_grad, second_stat = lax.psum(
        (router_part, jnp.sum(weighted_two * hidden_hat, axis=-1)), "tensor"
    )
    hidden_grad = scale_second * (weighted_two - hidden_hat * (second_stat / full_width)[:, None])
    branch_grad = (router[:, None] * cot_float + hidden_grad).astype(bf16)
    branch_full = lax.all_gather(branch_grad, "tensor", axis=1, tiled=True)
    grad_output = jnp.einsum("re,rd->ed", attended, branch_full, preferred_element_type=f32)
    attended_grad = jnp.einsum(
        "rd,ed->re", branch_full, w_output, preferred_element_type=f32
    ).astype(bf16)
    attended_grad = attended_grad.reshape(seq_local, capacity, -1, head_dim)
    scores = attend_scores(queries, key_rows)
    attend_prob = jnp.exp(scores - log_total)
    prob_grad = jnp.einsum("sqhe,skhe->shqk", attended_grad, value_rows, preferred_element_type=f32)
    row_dot = jnp.sum(attend_prob * prob_grad, axis=-1, keepdims=True)
    score_grad = (attend_prob * (prob_grad - row_dot)).astype(bf16)
    query_grad = (
        jnp.einsum("shqk,skhe->sqhe", score_grad, key_rows, preferred_element_type=f32)
        * score_scale
    )
    key_grad = (
        jnp.einsum("shqk,sqhe->skhe", score_grad, queries, preferred_element_type=f32) * score_scale
    )
    value_grad = jnp.einsum(
        "shqk,sqhe->skhe", attend_prob.astype(bf16), attended_grad, preferred_element_type=f32
    )
    project_grad = jnp.stack([query_grad, key_grad, value_grad]).astype(bf16).reshape(3, routed, -1)
    grad_project = jnp.einsum("rd,cre->cde", normed, project_grad, preferred_element_type=f32)
    normed_part = jnp.einsum("cre,cde->rd", project_grad, w_project, preferred_element_type=f32)
    normed_grad = lax.psum_scatter(normed_part, "tensor", scatter_dimension=1, tiled=True)
    rows_hat = rows_float * scale_first
    weighted_first = normed_grad * first_local
    grad_gain_first = jnp.sum(normed_grad * rows_hat, axis=0)
    first_stat = lax.psum(jnp.sum(weighted_first * rows_hat, axis=-1), "tensor")
    first_grad = scale_first * (weighted_first - rows_hat * (first_stat / full_width)[:, None])
    rows_grad = cot_float + hidden_grad + first_grad + router_grad[:, None] * router_local
    grad_router = jnp.sum(router_grad[:, None] * rows_float, axis=0)
    input_grad = out_grad.at[flat_rows].set(rows_grad.astype(bf16))
    summed = lax.psum(
        (
            grad_project,
            grad_output,
            grad_expand,
            grad_reduce,
            grad_gain_first,
            grad_gain_second,
            grad_router,
        ),
        "dp",
    )
    return (
        layer_out,
        input_grad,
        summed[0],
        summed[1],
        summed[2],
        summed[3],
        summed[4],
        summed[5],
        summed[6],
    )


def solution(mesh):
    return jax.shard_map(
        shards,
        mesh=mesh,
        in_specs=(
            P("dp", "tensor"),
            P("dp", "tensor"),
            P("dp", None),
            P("dp"),
            P(None, None, "tensor"),
            P("tensor", None),
            P(None, "tensor"),
            P("tensor", None),
            P(),
            P(),
            P(),
        ),
        out_specs=(
            P("dp", "tensor"),
            P("dp", "tensor"),
            P(None, None, "tensor"),
            P("tensor", None),
            P(None, "tensor"),
            P("tensor", None),
            P("tensor"),
            P("tensor"),
            P("tensor"),
        ),
        check_vma=False,
    )
```

profile of v0, /device:TPU:0, one launch (start us, length us, event | category | flops | bytes accessed | tf_op | source)
XLA Modules:
  0.0 1447.2 jit_solution(17592062476433951982)
XLA Ops:
  7.2 14.7 %copy.107 = bf16[16384,512]{1,0:T(8,128)(2,1)} copy(bf16[16384,512]{1,0:T(8,128)(2,1)} %param.11) | data formatting | bytes 33554432
  31.1 17.2 %gather_fusion = bf16[2048,512]{1,0:T(8,128)(2,1)} fusion(bf16[16384,512]{1,0:T(8,128)(2,1)} %copy.107, s32[2048]{0:T(1024)S(1)} %broadcast_clamp_fusion), kind=kCustom, calls=%fused_computation | custom fusion | bytes 4202496 | tf_op jit(solution)/shard_map/gather | solution.py:48
  49.2 11.8 gather_fusion.1
  62.4 45.6 %all-gather.11.cloned.1.call-done = bf16[2048,1024]{1,0:T(8,128)(2,1)} async-done(((bf16[2048,512]{1,0:T(8,128)(2,1)}), bf16[2048,1024]{1,0:T(8,128)(2,1)}) %all-gather.11.cloned.1.call-update) | async-done | bytes 4194320 | tf_op jit(solution)/shard_map/all_gather | solution.py:109
  155.8 10.9 fusion.47
  166.8 9.8 fusion.7
  176.5 9.4 convert_bitcast_fusion.2
  189.3 14.9 %fusion.49 = f32[2048,1024]{0,1:T(8,128)} fusion(bf16[2048,512]{0,1:T(8,128)(2,1)S(1)} %bitcast.71, bf16[512,1024]{1,0:T(8,128)(2,1)S(1)} %copy-done.38), kind=kOutput, calls=%fused_computation.93 | convolution fusion | flops 2147483648 | bytes 11534336 | tf_op jit(solution)/shard_map/dot_general | solution.py:82
  208.3 95.4 %reduce-scatter.5.cloned.1.call-done = f32[2048,512]{0,1:T(8,128)} async-done(((f32[2048,1024]{0,1:T(8,128)}), f32[2048,512]{0,1:T(8,128)}) %reduce-scatter.5.cloned.1.call-update) | async-done | bytes 4194320 | tf_op jit(solution)/shard_map/reduce_scatter | solution.py:83
  317.1 17.2 %gather_fusion.2 = bf16[2048,512]{1,0:T(8,128)(2,1)} fusion(bf16[16384,512]{1,0:T(8,128)(2,1)} %copy.108, s32[2048]{0:T(1024)S(1)} %broadcast_clamp_fusion), kind=kCustom, calls=%fused_computation.2 | custom fusion | bytes 4202496 | tf_op jit(solution)/shard_map/gather | solution.py:49
  341.7 32.2 %all-gather.7.cloned.1.call-done = bf16[2048,1024]{0,1:T(8,128)(2,1)} async-done(((bf16[2048,512]{0,1:T(8,128)(2,1)}), bf16[2048,1024]{0,1:T(8,128)(2,1)}) %all-gather.7.cloned.1.call-update) | async-done | bytes 4194320 | tf_op jit(solution)/shard_map/all_gather | solution.py:88
  373.9 15.3 %fusion.50 = f32[2048,2048]{1,0:T(8,128)} fusion(bf16[2048,1024]{0,1:T(8,128)(2,1)} %all-gather.7.cloned.1.call-done, bf16[1024,2048]{1,0:T(8,128)(2,1)} %param.17), kind=kOutput, calls=%fused_computation.94 | convolution fusion | flops 8589934592 | bytes 25165824 | tf_op jit(solution)/shard_map/dot_general | solution.py:89
  389.2 42.9 %all-gather.13.cloned.1.call-done = bf16[2048,1024]{0,1:T(8,128)(2,1)} async-done(((bf16[2048,512]{0,1:T(8,128)(2,1)}), bf16[2048,1024]{0,1:T(8,128)(2,1)}) %all-gather.13.cloned.1.call-update) | async-done | bytes 4194320 | tf_op jit(solution)/shard_map/all_gather | solution.py:136
  432.1 26.3 %fusion.6 = bf16[2048,2048]{1,0:T(8,128)(2,1)} fusion(f32[2048,2048]{1,0:T(8,128)} %fusion.50, bf16[2048,1024]{1,0:T(8,128)(2,1)} %param.18, bf16[2048,1024]{0,1:T(8,128)(2,1)} %all-gather.13.cloned.1.call-done, f32[2048]{0:T(1024)S(1)} %bitcast.76), kind=kOutput, calls=%fused_computation.13 | convolution fusion | flops 8680112128 | bytes 33562624 | tf_op jit(solution)/shard_map/rd,fd->rf/dot_general | solution.py:159
  458.4 14.9 %fusion.51 = f32[2048,1024]{0,1:T(8,128)} fusion(bf16[2048,2048]{1,0:T(8,128)(2,1)} %fusion.6, bf16[1024,2048]{1,0:T(8,128)(2,1)} %param.17), kind=kOutput, calls=%fused_computation.95 | convolution fusion | flops 8589934592 | bytes 20971520 | tf_op jit(solution)/shard_map/rf,df->rd/dot_general | solution.py:163
  473.4 19.6 %fusion.13 = (f32[2048]{0:T(1024)S(1)}, bf16[2048,1024]{0,1:T(8,128)(2,1)}) fusion(bf16[2048,1024]{0,1:T(8,128)(2,1)} %all-gather.13.cloned.1.call-done, f32[2048,1024]{0,1:T(8,128)} %fusion.49, bf16[2048,1024]{1,0:T(8,128)(2,1)} %param.18, f32[2048,2048]{1,0:T(8,128)} %fusion.50), kind=kOutput, calls=%fused_computation.31 | convolution fusion | flops 8638167040 | bytes 37756928 | tf_op jit(solution)/shard_map/dot_general | solution.py:127
  498.4 74.6 %reduce-scatter.9.cloned.1.call-done = f32[2048,512]{0,1:T(8,128)} async-done(((f32[2048,1024]{0,1:T(8,128)}), f32[2048,512]{0,1:T(8,128)}) %reduce-scatter.9.cloned.1.call-update) | async-done | bytes 4194320 | tf_op jit(solution)/shard_map/reduce_scatter | solution.py:164
  583.6 46.5 %reduce-scatter.7.cloned.1.call-done = bf16[2048,512]{0,1:T(8,128)(2,1)} async-done(((bf16[2048,1024]{0,1:T(8,128)(2,1)}), bf16[2048,512]{0,1:T(8,128)(2,1)}) %reduce-scatter.7.cloned.1.call-update) | async-done | bytes 2097168 | tf_op jit(solution)/shard_map/reduce_scatter | solution.py:128
  638.0 14.7 %fusion.53 = f32[1024,2048]{1,0:T(8,128)} fusion(bf16[2048,1024]{0,1:T(8,128)(2,1)} %all-gather.7.cloned.1.call-done, bf16[2048,2048]{1,0:T(8,128)(2,1)} %fusion.6), kind=kOutput, calls=%fused_computation.97 | convolution fusion | flops 8589934592 | bytes 20971520 | tf_op jit(solution)/shard_map/rd,rf->df/dot_general | solution.py:162
  652.7 17.2 %fusion.33 = f32[2048,1024]{1,0:T(8,128)} fusion(bf16[2048,1024]{0,1:T(8,128)(2,1)S(1)} %copy-done.36, f32[2048]{0:T(1024)S(1)} %bitcast.78, f32[2048,2048]{1,0:T(8,128)} %fusion.50), kind=kOutput, calls=%fused_computation.65 | convolution fusion | flops 8633974784 | bytes 29368320 | tf_op jit(solution)/shard_map/rf,rd->fd/dot_general | solution.py:158
  670.0 24.8 %all-gather.9.cloned.1.call-done = bf16[2048,1024]{0,1:T(8,128)(2,1)} async-done(((bf16[2048,512]{0,1:T(8,128)(2,1)}), bf16[2048,1024]{0,1:T(8,128)(2,1)}) %all-gather.9.cloned.1.call-update) | async-done | bytes 4194320 | tf_op jit(solution)/shard_map/all_gather | solution.py:173
  712.4 10.6 convert_bitcast_fusion.1
  723.0 10.9 multiply_reduce_fusion
  734.0 11.9 multiply_convert_fusion
  798.1 8.8 convolution_bitcast_fusion.1
  806.9 11.0 convolution_bitcast_fusion
  822.7 25.8 %scatter_fusion = bf16[16384,512]{1,0:T(8,128)(2,1)} fusion(bf16[16384,512]{1,0:T(8,128)(2,1)} %copy.107, s32[2048]{0:T(1024)S(1)} %bitcast.74, bf16[2048,512]{1,0:T(8,128)(2,1)} %copy.50), kind=kCustom, calls=%fused_computation.3 | custom fusion | bytes 6299648 | tf_op jit(solution)/shard_map/scatter | solution.py:133
  848.5 395.3 %all-reduce.4.cloned.1.call-done = (f32[3,1024,512]{1,2,0:T(8,128)}, f32[512,1024]{1,0:T(8,128)}, f32[1024,2048]{1,0:T(8,128)}, f32[2048,1024]{1,0:T(8,128)}) async-done(((f32[3,1024,512]{1,2,0:T(8,128)}, f32[512,1024]{1,0:T(8,128)}, f32[1024,2048]{1,0:T(8,128)}, f32[2048,1024]{1,0:T(8,128)}), (f32[3,1024,512]{1,2,0:T(8,128)}, f32[512,1024]{1,0:T(8,128)}, f32[1024,2048]{1,0:T(8,128)}, ...) | async-done | bytes 25165840 | tf_op jit(solution)/shard_map/psum | solution.py:206
  1250.4 95.3 %reduce-scatter.11.cloned.1.call-done = f32[2048,512]{0,1:T(8,128)} async-done(((f32[2048,1024]{0,1:T(8,128)}), f32[2048,512]{0,1:T(8,128)}) %reduce-scatter.11.cloned.1.call-update) | async-done | bytes 4194320 | tf_op jit(solution)/shard_map/reduce_scatter | solution.py:197
  1354.7 8.3 fusion.23
  1366.9 25.6 %scatter_fusion.1 = bf16[16384,512]{1,0:T(8,128)(2,1)} fusion(bf16[16384,512]{1,0:T(8,128)(2,1)} %copy.108, s32[2048]{0:T(1024)S(1)} %bitcast.75, bf16[2048,512]{1,0:T(8,128)(2,1)} %copy.70), kind=kCustom, calls=%fused_computation.4 | custom fusion | bytes 6299648 | tf_op jit(solution)/shard_map/scatter | solution.py:205
  1392.6 33.0 %all-reduce = (f32[512]{0:T(512)}, f32[512]{0:T(512)}, f32[512]{0:T(512)}) all-reduce(f32[512]{0:T(512)S(1)} %get-tuple-element.29, f32[512]{0:T(512)S(1)} %copy-done.27, f32[512]{0:T(512)S(1)} %copy-done.28), channel_id=1, replica_groups=mesh['dp'=16,'tensor'=2] {'dp'}, use_global_device_ids=true, to_apply=%region_23.24 | all-reduce | flops 1536 | bytes 12288 | tf_op jit(solution)/shard_map/psum | solution.py:206
  (163 shorter events, 220.0 us)
Async XLA Ops:
  7.2 104.0 %copy-start = (bf16[3,1024,512]{2,1,0:T(8,128)(2,1)S(1)}, bf16[3,1024,512]{2,1,0:T(8,128)(2,1)}, u32[]{:S(2)}) copy-start(bf16[3,1024,512]{2,1,0:T(8,128)(2,1)} %param.15) | copy-start | bytes 9437188
  7.2 100.8 %all-gather.11.cloned.1.call-start = ((), (), s32[]{:S(2)}) async-start(), calls=%async_computation.10 | async-start | bytes 6291456 | tf_op jit(solution)/shard_map/all_gather | solution.py:109
  7.2 17.0 %copy-start.7 = (bf16[16384,512]{1,0:T(8,128)(2,1)S(1)}, bf16[16384,512]{1,0:T(8,128)(2,1)}, u32[]{:S(2)}) copy-start(bf16[16384,512]{1,0:T(8,128)(2,1)} %param.12) | copy-start | bytes 50331652
  24.3 6.2 copy-start.24
  31.1 17.3 %copy-start.29 = (bf16[1024]{0:T(1024)(128)(2,1)S(1)}, bf16[1024]{0:T(1024)(128)(2,1)}, u32[]{:S(2)}) copy-start(bf16[1024]{0:T(1024)(128)(2,1)} %param.19) | copy-start | bytes 6148
  48.4 255.4 %reduce-scatter.5.cloned.1.call-start = ((), (), s32[]{:S(2)}) async-start(), calls=%async_computation.4 | async-start | bytes 12582912 | tf_op jit(solution)/shard_map/reduce_scatter | solution.py:83
  49.2 62.0 %copy-start.33 = (f32[1024]{0:T(1024)}, f32[1024]{0:T(1024)S(1)}, u32[]{:S(2)}) copy-start(f32[1024]{0:T(1024)S(1)} %convert_element_type.91) | copy-start | bytes 12292
  111.4 7.6 copy-start.18
  204.2 169.7 %all-gather.7.cloned.1.call-start = ((), (), s32[]{:S(2)}) async-start(), calls=%async_computation.5 | async-start | bytes 6291456 | tf_op jit(solution)/shard_map/all_gather | solution.py:88
  208.3 421.8 %copy-start.25 = (f32[512]{0:T(512)}, f32[512]{0:T(512)S(1)}, u32[]{:S(2)}) copy-start(f32[512]{0:T(512)S(1)} %dynamic-slice_convert_fusion.2) | copy-start | bytes 6148
  312.2 317.9 %copy-start.14 = (f32[2048]{0:T(1024)}, f32[2048]{0:T(1024)S(1)}, u32[]{:S(2)}) copy-start(f32[2048]{0:T(1024)S(1)} %add_rsqrt_fusion) | copy-start | bytes 24580
  317.1 115.0 %all-gather.13.cloned.1.call-start = ((), (), s32[]{:S(2)}) async-start(), calls=%async_computation.11 | async-start | bytes 6291456 | tf_op jit(solution)/shard_map/all_gather | solution.py:136
  338.3 234.7 %reduce-scatter.9.cloned.1.call-start = ((), (), s32[]{:S(2)}) async-start(), calls=%async_computation.7 | async-start | bytes 12582912 | tf_op jit(solution)/shard_map/reduce_scatter | solution.py:164
  473.3 156.8 %reduce-scatter.7.cloned.1.call-start = ((), (), s32[]{:S(2)}) async-start(), calls=%async_computation.6 | async-start | bytes 6291456 | tf_op jit(solution)/shard_map/reduce_scatter | solution.py:128
  493.0 201.8 %all-gather.9.cloned.1.call-start = ((), (), s32[]{:S(2)}) async-start(), calls=%async_computation.8 | async-start | bytes 6291456 | tf_op jit(solution)/shard_map/all_gather | solution.py:173
  498.4 80.3 %copy-start.20 = (f32[2048]{0:T(1024)}, f32[2048]{0:T(1024)S(1)}, u32[]{:S(2)}) copy-start(f32[2048]{0:T(1024)S(1)} %psum.83) | copy-start | bytes 24580
  583.6 54.3 %copy-start.22 = (f32[2048]{0:T(1024)}, f32[2048]{0:T(1024)S(1)}, u32[]{:S(2)}) copy-start(f32[2048]{0:T(1024)S(1)} %broadcast_multiply_fusion.1) | copy-start | bytes 24580
  637.9 605.9 %all-reduce.4.cloned.1.call-start = ((), (), s32[]{:S(2)}) async-start(), calls=%async_computation.12 | async-start | bytes 50331648 | tf_op jit(solution)/shard_map/psum | solution.py:206
  638.0 14.7 %copy-start.36 = (bf16[2048,1024]{0,1:T(8,128)(2,1)S(1)}, bf16[2048,1024]{0,1:T(8,128)(2,1)}, u32[]{:S(2)}) copy-start(bf16[2048,1024]{0,1:T(8,128)(2,1)} %all-gather.13.cloned.1.call-done) | copy-start | bytes 12582916
  712.4 10.6 copy-start.5
  712.4 10.6 copy-start.8
  734.0 11.9 copy-start.6
  792.9 5.2 copy-start.34
  806.9 538.8 %reduce-scatter.11.cloned.1.call-start = ((), (), s32[]{:S(2)}) async-start(), calls=%async_computation.9 | async-start | bytes 12582912 | tf_op jit(solution)/shard_map/reduce_scatter | solution.py:197
  1250.4 104.2 %copy-start.15 = (f32[2048]{0:T(1024)S(1)}, f32[2048]{0:T(1024)}, u32[]{:S(2)}) copy-start(f32[2048]{0:T(1024)} %copy-done.14) | copy-start | bytes 24580
  1250.4 104.2 %copy-start.21 = (f32[2048]{0:T(1024)S(1)}, f32[2048]{0:T(1024)}, u32[]{:S(2)}) copy-start(f32[2048]{0:T(1024)} %copy-done.20) | copy-start | bytes 24580
  1250.4 104.2 %copy-start.23 = (f32[2048]{0:T(1024)S(1)}, f32[2048]{0:T(1024)}, u32[]{:S(2)}) copy-start(f32[2048]{0:T(1024)} %copy-done.22) | copy-start | bytes 24580
  1250.4 104.3 %copy-start.26 = (f32[512]{0:T(512)S(1)}, f32[512]{0:T(512)}, u32[]{:S(2)}) copy-start(f32[512]{0:T(512)} %copy-done.25) | copy-start | bytes 6148
  1366.9 25.7 %copy-start.27 = (f32[512]{0:T(512)S(1)}, f32[512]{0:T(512)}, u32[]{:S(2)}) copy-start(f32[512]{0:T(512)} %get-tuple-element.27) | copy-start | bytes 6148
  1366.9 25.7 %copy-start.28 = (f32[512]{0:T(512)S(1)}, f32[512]{0:T(512)}, u32[]{:S(2)}) copy-start(f32[512]{0:T(512)} %get-tuple-element.31) | copy-start | bytes 6148
  1425.5 11.4 slice-start
  1428.8 8.0 slice-start.1
  (18 other events, 51.4 us)
Sparse Core Ops, SparseCore 0:
  48.5 59.4 all-gather.10
  204.4 99.3 reduce-scatter.4
  317.2 56.7 all-gather.6
  375.3 56.7 all-gather.12
  473.5 99.4 reduce-scatter.8
  575.7 54.3 reduce-scatter.6
  638.0 56.7 all-gather.8
  807.0 436.7 all-reduce.3
  1246.7 98.9 reduce-scatter.10
where the time goes:
time: 1460 us; the launch traced here: 1450 us
  waiting for transfers between devices  853 us (58%)
  local copies, waits for them, and re-layouts  253 us (17%)
  matrix products  212 us (15%)
  other arithmetic  60.7 us (4%)
  blocking collectives  53.2 us (4%)
  between operations  14.7 us (1%)
    psum x1, waiting for transfers between devices, shards(): lax.psum((grad_project, grad_output, grad_expand, grad_reduce, grad_gain_...  395 us
    reduce_scatter x1, waiting for transfers between devices, forward_rows(): lax.psum_scatter(attn_part, 'tensor', scatter_dimension=1, tiled=True)  95.4 us
    reduce_scatter x1, waiting for transfers between devices, shards(): lax.psum_scatter(normed_part, 'tensor', scatter_dimension=1, tiled=True)  95.3 us
    reduce_scatter x1, waiting for transfers between devices, shards(): lax.psum_scatter(normed_two_part, 'tensor', scatter_dimension=1, tiled=True)  74.6 us
    unnamed x93, local copies, waits for them, and re-layouts  55.3 us
    reduce_scatter x1, waiting for transfers between devices, shards(): lax.psum_scatter(mixer_part.astype(jnp.bfloat16), 'tensor', scatter_dimen...  46.5 us
    all_gather x1, waiting for transfers between devices, shards(): rows_full = lax.all_gather(rows_local, 'tensor', axis=1, tiled=True)  45.6 us
    all_gather x1, waiting for transfers between devices, shards(): lax.all_gather(cot_local, 'tensor', axis=1, tiled=True)  42.9 us
  transfers between devices with their start and end apart: 9, of which 9 were waited for; matrix products, arithmetic and copies ran while one was open for 11% of the time, Pallas kernels for 0%

commit v1 on v0

v1 whole, which is shorter than its diff:
```python
from functools import partial

import jax
import jax.numpy as jnp
from jax import lax
from jax.experimental import pallas as pl
from jax.experimental.pallas import tpu as pltpu
from jax.sharding import PartitionSpec as P

HEAD_DIM = 64
F32 = jnp.float32
BF16 = jnp.bfloat16
NT = (((1,), (1,)), ((), ()))
TN = (((0,), (0,)), ((), ()))
NN = (((1,), (0,)), ((), ()))


def dot(a, b, dims=NN, out=F32):
    return lax.dot_general(a, b, dims, preferred_element_type=F32).astype(out)


def params(limit=None):
    return pltpu.CompilerParams(dimension_semantics=("arbitrary",), vmem_limit_bytes=limit)


def gather_body(idx_ref, seg_ref, a_ref, b_ref, rows_ref, cots_ref, doc_ref):
    idx = idx_ref[0]
    length = a_ref.shape[1]
    hit = lax.broadcasted_iota(jnp.int32, (idx.shape[0], length), 1) == idx
    pick = hit.astype(F32).astype(BF16)
    rows_ref[0] = dot(pick, a_ref[0], out=BF16)
    cots_ref[0] = dot(pick, b_ref[0], out=BF16)
    doc_ref[0] = jnp.sum(jnp.where(hit, seg_ref[0], 0), axis=1, keepdims=True)


def gather_rows(layer_in, out_grad, route_index, segments):
    seqs, cap = route_index.shape
    width = layer_in.shape[1]
    length = layer_in.shape[0] // seqs
    big = pl.BlockSpec((1, length, width), lambda i: (i, 0, 0))
    small = pl.BlockSpec((1, cap, width), lambda i: (i, 0, 0))
    column = pl.BlockSpec((1, cap, 1), lambda i: (i, 0, 0))
    return pl.pallas_call(
        gather_body,
        grid=(seqs,),
        in_specs=[column, pl.BlockSpec((1, 1, length), lambda i: (i, 0, 0)), big, big],
        out_specs=[small, small, column],
        out_shape=[
            jax.ShapeDtypeStruct((seqs, cap, width), BF16),
            jax.ShapeDtypeStruct((seqs, cap, width), BF16),
            jax.ShapeDtypeStruct((seqs, cap, 1), jnp.int32),
        ],
        compiler_params=params(),
        name="gather_rows",
    )(
        route_index[:, :, None],
        segments.reshape(seqs, 1, length),
        layer_in.reshape(seqs, length, width),
        out_grad.reshape(seqs, length, width),
    )


def scatter_body(idx_ref, new_ref, a_ref, out_ref):
    idx = idx_ref[0]
    length = a_ref.shape[1]
    hit = lax.broadcasted_iota(jnp.int32, (length, idx.shape[1]), 0) == idx
    place = hit.astype(F32)
    routed = jnp.max(place, axis=1, keepdims=True) > 0.5
    moved = dot(place.astype(BF16), new_ref[0])
    out_ref[0] = jnp.where(routed, moved, a_ref[0].astype(F32)).astype(BF16)


def scatter_rows(base, rows, route_index):
    seqs, cap = route_index.shape
    width = base.shape[1]
    length = base.shape[0] // seqs
    big = pl.BlockSpec((1, length, width), lambda i: (i, 0, 0))
    out = pl.pallas_call(
        scatter_body,
        grid=(seqs,),
        in_specs=[
            pl.BlockSpec((1, 1, cap), lambda i: (i, 0, 0)),
            pl.BlockSpec((1, cap, width), lambda i: (i, 0, 0)),
            big,
        ],
        out_specs=big,
        out_shape=jax.ShapeDtypeStruct((seqs, length, width), BF16),
        compiler_params=params(),
        name="scatter_rows",
    )(route_index[:, None, :], rows, base.reshape(seqs, length, width))
    return out.reshape(base.shape)


def probs_of(query, key, allowed):
    scores = dot(query, key, NT) * HEAD_DIM ** (-0.5)
    scores = jnp.where(allowed, scores, -1e30)
    expo = jnp.exp(scores - jnp.max(scores, axis=1, keepdims=True))
    return expo / jnp.sum(expo, axis=1, keepdims=True)


def allowed_of(pos_c, pos_r, doc_c, doc_r):
    return (pos_r[0] <= pos_c[0]) & (doc_r[0] == doc_c[0])


def attend_body(pos_c, pos_r, doc_c, doc_r, qkv_ref, out_ref):
    allowed = allowed_of(pos_c, pos_r, doc_c, doc_r)
    for head in range(qkv_ref.shape[2] // HEAD_DIM):
        cols = slice(head * HEAD_DIM, (head + 1) * HEAD_DIM)
        probs = probs_of(qkv_ref[0, :, cols], qkv_ref[1, :, cols], allowed)
        out_ref[:, cols] = dot(probs.astype(BF16), qkv_ref[2, :, cols], out=BF16)


def attend_back_body(pos_c, pos_r, doc_c, doc_r, qkv_ref, grad_ref, out_ref):
    allowed = allowed_of(pos_c, pos_r, doc_c, doc_r)
    scale = HEAD_DIM ** (-0.5)
    for head in range(qkv_ref.shape[2] // HEAD_DIM):
        cols = slice(head * HEAD_DIM, (head + 1) * HEAD_DIM)
        query, key, value = (qkv_ref[c, :, cols] for c in range(3))
        grad = grad_ref[:, cols]
        probs = probs_of(query, key, allowed)
        prob_grad = dot(grad, value, NT)
        row_dot = jnp.sum(probs * prob_grad, axis=1, keepdims=True)
        score_grad = (probs * (prob_grad - row_dot)).astype(BF16)
        out_ref[0, :, cols] = (dot(score_grad, key) * scale).astype(BF16)
        out_ref[1, :, cols] = (dot(score_grad, query, TN) * scale).astype(BF16)
        out_ref[2, :, cols] = dot(probs.astype(BF16), grad, TN, BF16)


def attention(body, masks, cap, qkv, *more):
    width = qkv.shape[2]
    seqs = qkv.shape[1] // cap
    column = pl.BlockSpec((1, cap, 1), lambda i: (i, 0, 0))
    line = pl.BlockSpec((1, 1, cap), lambda i: (i, 0, 0))
    three = pl.BlockSpec((3, cap, width), lambda i: (0, i, 0))
    one = pl.BlockSpec((cap, width), lambda i: (i, 0))
    back = bool(more)
    return pl.pallas_call(
        body,
        grid=(seqs,),
        in_specs=[column, line, column, line, three] + [one] * len(more),
        out_specs=three if back else one,
        out_shape=jax.ShapeDtypeStruct(qkv.shape if back else qkv.shape[1:], BF16),
        compiler_params=params(),
        name="attend_back" if back else "attend",
    )(*masks, qkv, *more)


def gelu_parts(v):
    c = 0.7978845608028654
    th = jnp.tanh(c * (v + 0.044715 * (v * v * v)))
    half = 0.5 * (1.0 + th)
    slope = half + 0.5 * v * (1.0 - th * th) * (c * (1.0 + 3 * 0.044715 * (v * v)))
    return v * half, slope


def shards(
    sizes,
    layer_in,
    out_grad,
    route_index,
    segments,
    w_project,
    w_output,
    w_expand,
    w_reduce,
    gain_first,
    gain_second,
    w_router,
):
    copies, parts = sizes
    seq_local, cap = route_index.shape
    width = layer_in.shape[1]
    full = gain_first.shape[0]
    own_seqs = seq_local // parts
    own_rows = own_seqs * cap
    here = lax.axis_index("tensor")
    place = lax.axis_index("dp")
    core = place & 1

    def shift(value, step):
        return lax.ppermute(value, "tensor", [(s, (s + step) % parts) for s in range(parts)])

    def flip(value, bit):
        return lax.ppermute(value, "dp", [(s, s ^ bit) for s in range(copies)])

    def ordered(pieces):
        stacked = jnp.stack(pieces)
        if parts == 2:
            return [
                jnp.where(here == 0, pieces[0], pieces[1]),
                jnp.where(here == 0, pieces[1], pieces[0]),
            ]
        return [
            lax.dynamic_index_in_dim(stacked, (here - s) % parts, keepdims=False)
            for s in range(parts)
        ]

    def group_at(value, index):
        return lax.dynamic_index_in_dim(value, index % parts, keepdims=False)

    def to_rows(local):
        grouped = local.reshape(parts, own_rows, width)
        pieces = [group_at(grouped, here)]
        for k in range(1, parts):
            pieces.append(shift(group_at(grouped, here + k), k))
        return jnp.concatenate(ordered(pieces), axis=1)

    def to_features(value):
        blocks = value.reshape(own_rows, parts, width).transpose(1, 0, 2)
        pieces = [group_at(blocks, here)]
        for k in range(1, parts):
            pieces.append(shift(group_at(blocks, here + k), k))
        return jnp.concatenate(ordered(pieces), axis=0).reshape(seq_local, cap, width)

    def far(weight, k, axis):
        half = weight.shape[axis] // 2
        mine = lax.dynamic_slice_in_dim(weight, core * half, half, axis)
        mine = shift(mine, -k)
        other = flip(mine, 1)
        return jnp.where(
            core == 0,
            jnp.concatenate([mine, other], axis),
            jnp.concatenate([other, mine], axis),
        )

    def every(weight, axis):
        return [weight] + [far(weight, k, axis) for k in range(1, parts)]

    rows_local, cot_local, docs = gather_rows(layer_in, out_grad, route_index, segments)
    rows_in = to_rows(rows_local)
    project_all = every(w_project, 1)
    output_all = every(w_output, 0)
    cot_in = to_rows(cot_local)
    expand_all = every(w_expand, 0)
    reduce_all = every(w_reduce, 0)
    rows = rows_in.astype(F32)
    cot = cot_in.astype(F32)
    positions = group_at(route_index.reshape(parts, own_seqs, cap), here)
    docs = group_at(docs.reshape(parts, own_seqs, cap), here)
    masks = (positions[:, :, None], positions[:, None, :], docs[:, :, None], docs[:, None, :])
    gain_one = gain_first.astype(F32)
    gain_two = gain_second.astype(F32)
    router_row = w_router.astype(F32)

    router = jnp.sum(rows * router_row, axis=1, keepdims=True)
    scale_first = lax.rsqrt(jnp.mean(rows * rows, axis=1, keepdims=True) + 1e-06)
    normed = (rows * scale_first * gain_one).astype(BF16)
    qkv_all = [
        jnp.einsum("rd,cde->cre", normed, w, preferred_element_type=F32).astype(BF16)
        for w in project_all
    ]
    attended_all = [attention(attend_body, masks, cap, qkv) for qkv in qkv_all]
    attn_out = sum(dot(a, w) for a, w in zip(attended_all, output_all))
    hidden = rows + attn_out
    scale_second = lax.rsqrt(jnp.mean(hidden * hidden, axis=1, keepdims=True) + 1e-06)
    normed_two = (hidden * scale_second * gain_two).astype(BF16)
    mixer_grad = (router * cot).astype(BF16)
    activated_all = []
    slope_all = []
    for w in expand_all:
        act, slope = gelu_parts(dot(normed_two, w))
        activated_all.append(act.astype(BF16))
        slope_all.append(slope.astype(BF16))
    back_all = [
        (dot(mixer_grad, w, NT) * slope.astype(F32)).astype(BF16)
        for w, slope in zip(reduce_all, slope_all)
    ]
    reduce_grads = [dot(a, mixer_grad, TN, BF16) for a in activated_all]
    expand_grads = [dot(normed_two, g, TN, BF16) for g in back_all]

    def reduce_over(grads):
        step = grads[0].shape[0] // copies
        rest = grads[0].shape[1:]

        def add(a, b):
            return (a.astype(F32) + b.astype(F32)).astype(BF16)

        kept = []
        for grad in grads:
            blocks = grad.reshape(copies // 2, 2, step, *rest)
            mine = lax.dynamic_index_in_dim(blocks, core, 1, keepdims=False)
            other = lax.dynamic_index_in_dim(blocks, 1 - core, 1, keepdims=False)
            kept.append(add(mine, flip(other, 1)))
        total = kept[0]
        for k in range(1, parts):
            total = add(total, shift(kept[k], k))
        value = total
        bit = 2
        while bit < copies:
            value = value.reshape((value.shape[0] // 2, 2, step) + tuple(rest))
            mine = lax.dynamic_index_in_dim(value, (place // bit) & 1, 1, keepdims=False)
            other = lax.dynamic_index_in_dim(value, 1 - ((place // bit) & 1), 1, keepdims=False)
            value = add(mine, flip(other, bit))
            bit *= 2
        return value.reshape((step,) + tuple(rest))

    def collect(pieces):
        gathered = lax.all_gather(tuple(pieces), "dp", axis=0, tiled=True)
        return [g.astype(F32) for g in gathered]

    grad_reduce, grad_expand = collect([reduce_over(reduce_grads), reduce_over(expand_grads)])

    mixer_out = sum(dot(a, w) for a, w in zip(activated_all, reduce_all))
    branch = attn_out + mixer_out
    layer_rows = (rows + router * branch).astype(BF16)
    router_grad = jnp.sum(cot * branch, axis=1, keepdims=True)
    layer_out = scatter_rows(layer_in, to_features(layer_rows), route_index)

    two_grad = sum(dot(g, w, NT) for g, w in zip(back_all, expand_all))
    hidden_hat = hidden * scale_second
    weighted_two = two_grad * gain_two
    gain_two_part = jnp.sum(two_grad * hidden_hat, axis=0)
    stat_two = jnp.mean(weighted_two * hidden_hat, axis=1, keepdims=True)
    hidden_grad = scale_second * (weighted_two - hidden_hat * stat_two)
    branch_grad = (router * cot + hidden_grad).astype(BF16)
    output_grads = [dot(a, branch_grad, TN, BF16) for a in attended_all]
    back_heads = [dot(branch_grad, w, NT, BF16) for w in output_all]
    project_back = [
        attention(attend_back_body, masks, cap, qkv, g) for qkv, g in zip(qkv_all, back_heads)
    ]
    project_grads = [
        jnp.einsum("rd,cre->cde", normed, g, preferred_element_type=F32)
        .astype(BF16)
        .reshape(3 * full, -1)
        for g in project_back
    ]
    normed_grad = sum(
        dot(g[c], w[c], NT) for g, w in zip(project_back, project_all) for c in range(3)
    )
    rows_hat = rows * scale_first
    weighted_one = normed_grad * gain_one
    gain_one_part = jnp.sum(normed_grad * rows_hat, axis=0)
    stat_one = jnp.mean(weighted_one * rows_hat, axis=1, keepdims=True)
    first_grad = scale_first * (weighted_one - rows_hat * stat_one)
    rows_grad = cot + hidden_grad + first_grad + router_grad * router_row
    router_part = jnp.sum(router_grad * rows, axis=0)
    input_grad = scatter_rows(out_grad, to_features(rows_grad.astype(BF16)), route_index)

    project_sum, output_sum = collect([reduce_over(project_grads), reduce_over(output_grads)])
    grad_project = project_sum.reshape(3, full, -1)
    small = lax.psum(jnp.stack([gain_one_part, gain_two_part, router_part]), ("dp", "tensor"))
    small = lax.dynamic_slice_in_dim(small, here * width, width, 1)
    return (
        layer_out,
        input_grad,
        grad_project,
        output_sum,
        grad_expand,
        grad_reduce,
        small[0],
        small[1],
        small[2],
    )


def solution(mesh):
    return jax.shard_map(
        partial(shards, (mesh.shape["dp"], mesh.shape["tensor"])),
        mesh=mesh,
        in_specs=(
            P("dp", "tensor"),
            P("dp", "tensor"),
            P("dp", None),
            P("dp"),
            P(None, None, "tensor"),
            P("tensor", None),
            P(None, "tensor"),
            P("tensor", None),
            P(),
            P(),
            P(),
        ),
        out_specs=(
            P("dp", "tensor"),
            P("dp", "tensor"),
            P(None, None, "tensor"),
            P("tensor", None),
            P(None, "tensor"),
            P("tensor", None),
            P("tensor"),
            P("tensor"),
            P("tensor"),
        ),
        check_vma=False,
    )
```

time: 1460 us -> 894 us (0.61)
  waiting for transfers between devices: 853 us -> 310 us
  local copies, waits for them, and re-layouts: 253 us -> 71.7 us
  Pallas kernels: 0 us -> 121 us
  starting transfers between devices: 0.37 us -> 43.6 us
  matrix products: 212 us -> 197 us
    psum x1 -> x0, waiting for transfers between devices: 395 us -> none  [shards(): lax.psum((grad_project, grad_output, grad_expand, grad_reduce, grad_gain_...]
    reduce_scatter x4 -> x0, waiting for transfers between devices: 312 us -> none  [the longest x1 95.4 us: forward_rows(): lax.psum_scatter(attn_part, 'tensor', scatter_dimension=1, tiled=True)]
    ppermute x0 -> x36, waiting for transfers between devices: none -> 310 us  [the longest x12 190 us: shift(): lax.ppermute(value, 'tensor', [(s, (s + step) % parts) for s in range(par...]
    all_gather x4, waiting for transfers between devices: 145 us -> 0.01 us  [collect(): gathered = lax.all_gather(tuple(pieces), 'dp', axis=0, tiled=True)]
    pallas_call x0 -> x7, Pallas kernels: none -> 121 us  [the longest x4 69.5 us: attention(): pl.pallas_call(body, grid=(seqs,), in_specs=[column, line, column, line,...]
    gather x5 -> x0, local copies, waits for them, and re-layouts: 54.1 us -> none  [the longest x2 21.2 us: shards(): cot_local = out_grad[flat_rows]]
    scatter x2 -> x0, local copies, waits for them, and re-layouts: 51.5 us -> none  [the longest x1 25.8 us: shards(): layer_out = layer_in.at[flat_rows].set(layer_rows.astype(bf16))]
    ppermute x0 -> x36, starting transfers between devices: none -> 43.2 us  [the longest x24 27.1 us: flip(): return lax.ppermute(value, 'dp', [(s, s ^ bit) for s in range(copies)])]
  transfers between devices with their start and end apart: 9 -> 40, of which waited for: 9 -> 16; matrix products, arithmetic and copies ran while one was open for 11% -> 29% of each run, Pallas kernels for 0% -> 14%
where the time goes in v1:
time: 894 us; the launch traced here: 884 us
  waiting for transfers between devices  310 us (35%)
  matrix products  197 us (22%)
  Pallas kernels  121 us (14%)
  local copies, waits for them, and re-layouts  71.7 us (8%)
  other arithmetic  70.8 us (8%)
  blocking collectives  55 us (6%)
  starting transfers between devices  43.6 us (5%)
  between operations  15 us (2%)
    ppermute x12, waiting for transfers between devices, shift(): lax.ppermute(value, 'tensor', [(s, (s + step) % parts) for s in range(par...  190 us
    dot_general x24, matrix products, dot(): return lax.dot_general(a, b, dims, preferred_element_type=F32).astype(out)  172 us
    ppermute x24, waiting for transfers between devices, flip(): return lax.ppermute(value, 'dp', [(s, s ^ bit) for s in range(copies)])  120 us
    pallas_call x4, Pallas kernels, attention(): pl.pallas_call(body, grid=(seqs,), in_specs=[column, line, column, line,...  69.5 us
    psum x1, blocking collectives, shards(): lax.psum(jnp.stack([gain_one_part, gain_two_part, router_part]), ('dp', '...  55 us
    pallas_call x2, Pallas kernels, scatter_rows(): pl.pallas_call(scatter_body, grid=(seqs,), in_specs=[pl.BlockSpec((1, 1,...  33 us
    ppermute x24, starting transfers between devices, flip(): return lax.ppermute(value, 'dp', [(s, s ^ bit) for s in range(copies)])  27.1 us
    convert_element_type x20, other arithmetic, add(): return (a.astype(F32) + b.astype(F32)).astype(BF16)  25.5 us
  transfers between devices with their start and end apart: 40, of which 16 were waited for; matrix products, arithmetic and copies ran while one was open for 29% of the time, Pallas kernels for 14%

profile of v1, /device:TPU:0, one launch (start us, length us, event | category | flops | bytes accessed | tf_op | source)
XLA Modules:
  0.0 884.5 jit_solution(9391158636731169896)
XLA Ops:
  15.0 19.0 %gather_rows.1 = (bf16[8,256,512]{2,1,0:T(8,128)(2,1)}, bf16[8,256,512]{2,1,0:T(8,128)(2,1)}, s32[8,256,1]{2,1,0:T(8,128)}) custom-call(s32[8,256,1]{2,1,0:T(8,128)} %copy.69.idx_ref, s32[8,1,2048]{2,1,0:T(1,128)} %bitcast.294, bf16[8,2048,512]{2,1,0:T(8,128)(2,1)} %bitcast.246, bf16[8,2048,512]{2,1,0:T(8,128)(2,1)} %bitcast.244), custom_call_target="tpu_custom_call" | custom-call | tf_op jit(solution)/shard_map/gather_rows/pallas_call | solution.py:43
  59.4 22.8 %collective-permute-done.3 = bf16[256,1024]{1,0:T(8,128)(2,1)} collective-permute-done((bf16[256,1024]{1,0:T(8,128)(2,1)}, bf16[256,1024]{1,0:T(8,128)(2,1)}, u32[]{:S(2)}, u32[]{:S(2)}) %collective-permute-start.3) | collective-permute-done | bytes 524320 | tf_op jit(solution)/shard_map/ppermute | solution.py:181
  92.1 13.3 %attend.2 = bf16[1024,512]{1,0:T(8,128)(2,1)} custom-call(s32[4,256,1]{2,1,0:T(8,128)} %copy.73.pos_c, s32[4,1,256]{2,1,0:T(1,128)} %broadcast_in_dim.15.pos_r, s32[4,256,1]{2,1,0:T(8,128)} %copy.74.doc_c, s32[4,1,256]{2,1,0:T(1,128)} %broadcast_in_dim.17.doc_r, bf16[3,1024,512]{2,1,0:T(8,128)(2,1)} %convert_bitcast_fusion.3.qkv_ref), custom_call_target="tpu_custom_call" | custom-call | tf_op jit(solution)/shard_map/attend/pallas_call | solution.py:137
  105.5 88.3 %collective-permute-done.10 = bf16[1024,512]{0,1:T(8,128)(2,1)} collective-permute-done((bf16[1024,512]{0,1:T(8,128)(2,1)}, bf16[1024,512]{0,1:T(8,128)(2,1)}, u32[]{:S(2)}, u32[]{:S(2)}) %collective-permute-start.10) | collective-permute-done | bytes 1048608 | tf_op jit(solution)/shard_map/ppermute | solution.py:181
  211.0 13.3 %attend.3 = bf16[1024,512]{1,0:T(8,128)(2,1)} custom-call(s32[4,256,1]{2,1,0:T(8,128)} %copy.73.pos_c, s32[4,1,256]{2,1,0:T(1,128)} %broadcast_in_dim.15.pos_r, s32[4,256,1]{2,1,0:T(8,128)} %copy.74.doc_c, s32[4,1,256]{2,1,0:T(1,128)} %broadcast_in_dim.17.doc_r, bf16[3,1024,512]{2,1,0:T(8,128)(2,1)} %convert_bitcast_fusion.2.qkv_ref), custom_call_target="tpu_custom_call" | custom-call | tf_op jit(solution)/shard_map/attend/pallas_call | solution.py:137
  233.2 6.9 fusion.84
  240.2 12.7 %multiply_convert_fusion.1 = bf16[1024,2048]{1,0:T(8,128)(2,1)} fusion(bf16[2048,1024]{1,0:T(8,128)(2,1)S(1)} %copy-done.32, f32[1024,2048]{1,0:T(8,128)} %fusion.84, f32[1024]{0:T(1024)S(1)} %get-tuple-element.20, bf16[1024,512]{0,1:T(8,128)(2,1)S(1)} %copy-done.17, bf16[1024,512]{0,1:T(8,128)(2,1)S(1)} %copy-done.15), kind=kOutput, calls=%fused_computation.29 | convolution fusion | flops 4343201792 | bytes 18878464 | tf_op jit(solution)/shard_map/dot_general | solution.py:19
  252.9 10.3 %fusion.81 = f32[1024,1024]{0,1:T(8,128)} fusion(bf16[2048,1024]{1,0:T(8,128)(2,1)S(1)} %copy-done.32, f32[1024,2048]{1,0:T(8,128)} %fusion.84), kind=kOutput, calls=%fused_computation.203 | convolution fusion | flops 4313841664 | bytes 16777216 | tf_op jit(solution)/shard_map/dot_general | solution.py:19
  263.2 8.4 fusion.85
  271.6 11.5 %fusion.68 = f32[1024,2048]{1,0:T(8,128)} fusion(bf16[1024,1024]{0,1:T(8,128)(2,1)S(1)} %multiply_convert_fusion.4, bf16[512,2048]{1,0:T(8,128)(2,1)} %collective-permute-done.6, bf16[512,2048]{1,0:T(8,128)(2,1)} %collective-permute-done.5, pred[]{:T(512)S(6)} %eq.28), kind=kOutput, calls=%fused_computation.161 | convolution fusion | flops 4313841664 | bytes 14680065 | tf_op jit(solution)/shard_map/dot_general | solution.py:19
  283.1 15.0 %multiply_convert_fusion = bf16[1024,2048]{1,0:T(8,128)(2,1)} fusion(f32[1024,2048]{1,0:T(8,128)} %fusion.68, f32[1024]{0:T(1024)S(1)} %get-tuple-element.20, bf16[1024,1024]{1,0:T(8,128)(2,1)} %collective-permute-done.8, bf16[1024,1024]{1,0:T(8,128)(2,1)} %collective-permute-done.7, pred[]{:T(512)S(6)} %eq.28, bf16[1024,512]{0,1:T(8,128)(2,1)S(1)} %copy-done.17, ...), kind=kOutput, calls=%fused_computation.28 | convolution fusion | flops 4362076160 | bytes 18878464 | tf_op jit(solution)/shard_map/dot_general | solution.py:19
  298.1 8.5 convolution_convert_fusion.2
  306.6 13.5 %multiply_reduce_fusion = (f32[1024]{0:T(1024)}, f32[1024]{0:T(1024)S(1)}, f32[1024,1024]{0,1:T(8,128)}) fusion(f32[1024]{0:T(1024)S(1)} %add_rsqrt_fusion, f32[1024,1024]{0,1:T(8,128)S(1)} %get-tuple-element.40, bf16[1024,512]{0,1:T(8,128)(2,1)S(1)} %get-tuple-element.34, bf16[1024,512]{0,1:T(8,128)(2,1)S(1)} %get-tuple-element.33, ...), kind=kOutput, calls=%fused_computation.69 | convolution fusion | flops 4326422528 | bytes 23085056 | tf_op jit(solution)/shard_map/dot_general | solution.py:19
  320.1 19.2 %fusion.28 = (f32[1024]{0:T(1024)S(1)}, bf16[1024,1024]{0,1:T(8,128)(2,1)}, bf16[1024,1024]{0,1:T(8,128)(2,1)}) fusion(bf16[1024,512]{0,1:T(8,128)(2,1)} %get-tuple-element.30, bf16[1024,512]{0,1:T(8,128)(2,1)} %get-tuple-element.29, f32[1024]{0:T(1024)S(1)} %get-tuple-element.20, bf16[1024,512]{0,1:T(8,128)(2,1)S(1)} %get-tuple-element.34, ...), kind=kOutput, calls=%fused_computation.47 | convolution fusion | flops 4357880832 | bytes 33574912 | tf_op jit(solution)/shard_map/dot_general | solution.py:19
  351.4 21.3 %attend_back.3 = bf16[3,1024,512]{2,1,0:T(8,128)(2,1)} custom-call(s32[4,256,1]{2,1,0:T(8,128)} %copy.73.pos_c, s32[4,1,256]{2,1,0:T(1,128)} %broadcast_in_dim.15.pos_r, s32[4,256,1]{2,1,0:T(8,128)} %copy.74.doc_c, s32[4,1,256]{2,1,0:T(1,128)} %broadcast_in_dim.17.doc_r, bf16[3,1024,512]{2,1,0:T(8,128)(2,1)} %convert_bitcast_fusion.2.qkv_ref, ...), custom_call_target="tpu_custom_call" | custom-call | tf_op jit(solution)/shard_map/attend_back/pallas_call | solution.py:137
  372.7 21.5 %attend_back.2 = bf16[3,1024,512]{2,1,0:T(8,128)(2,1)} custom-call(s32[4,256,1]{2,1,0:T(8,128)} %copy.73.pos_c, s32[4,1,256]{2,1,0:T(1,128)} %broadcast_in_dim.15.pos_r, s32[4,256,1]{2,1,0:T(8,128)} %copy.74.doc_c, s32[4,1,256]{2,1,0:T(1,128)} %broadcast_in_dim.17.doc_r, bf16[3,1024,512]{2,1,0:T(8,128)(2,1)} %convert_bitcast_fusion.3.qkv_ref, ...), custom_call_target="tpu_custom_call" | custom-call | tf_op jit(solution)/shard_map/attend_back/pallas_call | solution.py:137
  395.5 8.3 convert_bitcast_fusion
  461.4 19.4 %collective-permute-done.14 = bf16[8,192,512]{2,1,0:T(8,128)(2,1)S(1)} collective-permute-done((bf16[8,192,512]{2,1,0:T(8,128)(2,1)S(1)}, bf16[8,192,512]{2,1,0:T(8,128)(2,1)S(1)}, u32[]{:S(2)}, u32[]{:S(2)}) %collective-permute-start.14) | collective-permute-done | bytes 1572896 | tf_op jit(solution)/shard_map/ppermute | solution.py:181
  506.0 9.2 %collective-permute-done.16 = bf16[2,192,512]{2,1,0:T(8,128)(2,1)S(1)} collective-permute-done((bf16[2,192,512]{2,1,0:T(8,128)(2,1)S(1)}, bf16[2,192,512]{2,1,0:T(8,128)(2,1)S(1)}, u32[]{:S(2)}, u32[]{:S(2)}) %collective-permute-start.16) | collective-permute-done | bytes 393248 | tf_op jit(solution)/shard_map/ppermute | solution.py:184
  534.4 25.0 %collective-permute-done.27 = bf16[4,64,2048]{2,1,0:T(8,128)(2,1)S(1)} collective-permute-done((bf16[4,64,2048]{2,1,0:T(8,128)(2,1)S(1)}, bf16[4,64,2048]{2,1,0:T(8,128)(2,1)S(1)}, u32[]{:S(2)}, u32[]{:S(2)}) %collective-permute-start.27) | collective-permute-done | bytes 1048608 | tf_op jit(solution)/shard_map/ppermute | solution.py:184
  562.9 22.9 %collective-permute-done.28 = bf16[2,64,2048]{2,1,0:T(8,128)(2,1)S(1)} collective-permute-done((bf16[2,64,2048]{2,1,0:T(8,128)(2,1)S(1)}, bf16[2,64,2048]{2,1,0:T(8,128)(2,1)S(1)}, u32[]{:S(2)}, u32[]{:S(2)}) %collective-permute-start.28) | collective-permute-done | bytes 524320 | tf_op jit(solution)/shard_map/ppermute | solution.py:184
  588.7 9.8 %convolution_convert_fusion = bf16[2048,1024]{1,0:T(8,128)(2,1)S(1)} fusion(f32[1024]{0:T(1024)S(1)} %get-tuple-element.20, bf16[1024,512]{0,1:T(8,128)(2,1)S(1)} %copy-done.18, bf16[1024,512]{0,1:T(8,128)(2,1)S(1)} %copy-done.16, f32[1024,2048]{1,0:T(8,128)} %fusion.68), kind=kOutput, calls=%fused_computation.78 | convolution fusion | flops 4322230272 | bytes 14684160 | tf_op jit(solution)/shard_map/dot_general | solution.py:19
  603.0 10.0 %convolution_convert_fusion.1 = bf16[2048,1024]{1,0:T(8,128)(2,1)S(1)} fusion(f32[1024]{0:T(1024)S(1)} %get-tuple-element.20, bf16[1024,512]{0,1:T(8,128)(2,1)} %get-tuple-element.30, bf16[1024,512]{0,1:T(8,128)(2,1)S(1)} %copy-done.16, f32[1024,2048]{1,0:T(8,128)} %fusion.84), kind=kOutput, calls=%fused_computation.79 | convolution fusion | flops 4322230272 | bytes 14684160 | tf_op jit(solution)/shard_map/dot_general | solution.py:19
  619.3 46.6 %collective-permute-done.32 = bf16[8,128,1024]{2,1,0:T(8,128)(2,1)S(1)} collective-permute-done((bf16[8,128,1024]{2,1,0:T(8,128)(2,1)S(1)}, bf16[8,128,1024]{2,1,0:T(8,128)(2,1)S(1)}, u32[]{:S(2)}, u32[]{:S(2)}) %collective-permute-start.32) | collective-permute-done | bytes 2097184 | tf_op jit(solution)/shard_map/ppermute | solution.py:181
  669.2 23.2 %collective-permute-done.33 = bf16[4,128,1024]{2,1,0:T(8,128)(2,1)S(1)} collective-permute-done((bf16[4,128,1024]{2,1,0:T(8,128)(2,1)S(1)}, bf16[4,128,1024]{2,1,0:T(8,128)(2,1)S(1)}, u32[]{:S(2)}, u32[]{:S(2)}) %collective-permute-start.33) | collective-permute-done | bytes 1048608 | tf_op jit(solution)/shard_map/ppermute | solution.py:184
  695.4 10.9 %collective-permute-done.34 = bf16[2,128,1024]{2,1,0:T(8,128)(2,1)S(1)} collective-permute-done((bf16[2,128,1024]{2,1,0:T(8,128)(2,1)S(1)}, bf16[2,128,1024]{2,1,0:T(8,128)(2,1)S(1)}, u32[]{:S(2)}, u32[]{:S(2)}) %collective-permute-start.34) | collective-permute-done | bytes 524320 | tf_op jit(solution)/shard_map/ppermute | solution.py:184
  707.2 12.4 %collective-permute-done.35 = bf16[1,128,1024]{2,1,0:T(8,128)(2,1)S(1)} collective-permute-done((bf16[1,128,1024]{2,1,0:T(8,128)(2,1)S(1)}, bf16[1,128,1024]{2,1,0:T(8,128)(2,1)S(1)}, u32[]{:S(2)}, u32[]{:S(2)}) %collective-permute-start.35) | collective-permute-done | bytes 262176 | tf_op jit(solution)/shard_map/ppermute | solution.py:184
  736.1 8.5 fusion.33
  744.6 7.4 fusion.27
  756.0 55.0 %psum.7 = f32[3,1024]{1,0:T(4,128)S(1)} all-reduce(f32[3,1024]{1,0:T(4,128)S(1)} %pad_maximum_fusion.4), channel_id=1, replica_groups=mesh['dp'=16,'tensor'=2] {'dp','tensor'}, use_global_device_ids=true, to_apply=%region_9.10 | all-reduce | flops 3072 | bytes 24576 | tf_op jit(solution)/shard_map/psum | solution.py:341
  822.9 16.5 %scatter_rows.3 = bf16[8,2048,512]{2,1,0:T(8,128)(2,1)} custom-call(s32[8,1,256]{2,1,0:T(1,128)} %broadcast_in_dim.12.idx_ref, bf16[8,256,512]{2,1,0:T(8,128)(2,1)} %bitcast.257, bf16[8,2048,512]{2,1,0:T(8,128)(2,1)} %bitcast.245), custom_call_target="tpu_custom_call" | custom-call | tf_op jit(solution)/shard_map/scatter_rows/pallas_call | solution.py:78
  839.3 16.5 %scatter_rows.2 = bf16[8,2048,512]{2,1,0:T(8,128)(2,1)} custom-call(s32[8,1,256]{2,1,0:T(1,128)} %broadcast_in_dim.12.idx_ref, bf16[8,256,512]{2,1,0:T(8,128)(2,1)} %bitcast.256, bf16[8,2048,512]{2,1,0:T(8,128)(2,1)} %bitcast.247), custom_call_target="tpu_custom_call" | custom-call | tf_op jit(solution)/shard_map/scatter_rows/pallas_call | solution.py:78
  (268 shorter events, 262.3 us)
Async XLA Ops:
  7.2 848.6 %all-gather.11.cloned.1.call-start = ((), (), s32[]{:S(2)}) async-start(), calls=%async_computation.1 | async-start | bytes 1114112 | tf_op jit(solution)/shard_map/all_gather | solution.py:298
  10.0 76.4 %collective-permute-start.1 = (bf16[3,512,512]{2,1,0:T(8,128)(2,1)}, bf16[3,512,512]{2,1,0:T(8,128)(2,1)}, u32[]{:S(2)}, u32[]{:S(2)}) collective-permute-start(bf16[3,512,512]{2,1,0:T(8,128)(2,1)} %constant_dynamic-slice_fusion.10), channel_id=1, source_target_pairs={{0,1},{1,0},{2,3},{3,2},{4,5},{5,4},{6,7},{7,6},{8,9},{9,8},{10,11... | collective-permute-start | bytes 4718600 | tf_op jit(solution)/shard_map/ppermute | solution.py:181
  40.0 44.2 %collective-permute-start = (bf16[1024,512]{0,1:T(8,128)(2,1)}, bf16[1024,512]{0,1:T(8,128)(2,1)}, u32[]{:S(2)}, u32[]{:S(2)}) collective-permute-start(bf16[1024,512]{0,1:T(8,128)(2,1)} %bitcast.287), channel_id=1, source_target_pairs={{0,1},{1,0},{2,3},{3,2},{4,5},{5,4},{6,7},{7,6},{8,9},{9,8},{10,11... | collective-permute-start | bytes 3145736 | tf_op jit(solution)/shard_map/ppermute | solution.py:181
  40.8 41.4 %collective-permute-start.3 = (bf16[256,1024]{1,0:T(8,128)(2,1)}, bf16[256,1024]{1,0:T(8,128)(2,1)}, u32[]{:S(2)}, u32[]{:S(2)}) collective-permute-start(bf16[256,1024]{1,0:T(8,128)(2,1)} %constant_dynamic-slice_fusion.9), channel_id=1, source_target_pairs={{0,1},{1,0},{2,3},{3,2},{4,5},{5,4},{6,7},{7,6},{8,9},{9,8},{10,11... | collective-permute-start | bytes 1572872 | tf_op jit(solution)/shard_map/ppermute | solution.py:181
  46.1 153.9 %collective-permute-start.7 = (bf16[1024,1024]{1,0:T(8,128)(2,1)}, bf16[1024,1024]{1,0:T(8,128)(2,1)}, u32[]{:S(2)}, u32[]{:S(2)}) collective-permute-start(bf16[1024,1024]{1,0:T(8,128)(2,1)} %constant_dynamic-slice_fusion.7), channel_id=1, source_target_pairs={{0,1},{1,0},{2,3},{3,2},{4,5},{5,4},{6,7},{7,6},{8,9},{9,8},{10,11... | collective-permute-start | bytes 6291464 | tf_op jit(solution)/shard_map/ppermute | solution.py:181
  47.6 152.4 %collective-permute-start.5 = (bf16[512,2048]{1,0:T(8,128)(2,1)}, bf16[512,2048]{1,0:T(8,128)(2,1)}, u32[]{:S(2)}, u32[]{:S(2)}) collective-permute-start(bf16[512,2048]{1,0:T(8,128)(2,1)} %constant_dynamic-slice_fusion.8), channel_id=1, source_target_pairs={{0,1},{1,0},{2,3},{3,2},{4,5},{5,4},{6,7},{7,6},{8,9},{9,8},{10,11... | collective-permute-start | bytes 6291464 | tf_op jit(solution)/shard_map/ppermute | solution.py:181
  82.2 111.5 %collective-permute-start.10 = (bf16[1024,512]{0,1:T(8,128)(2,1)}, bf16[1024,512]{0,1:T(8,128)(2,1)}, u32[]{:S(2)}, u32[]{:S(2)}) collective-permute-start(bf16[1024,512]{0,1:T(8,128)(2,1)} %bitcast.288), channel_id=1, source_target_pairs={{0,1},{1,0},{2,3},{3,2},{4,5},{5,4},{6,7},{7,6},{8,9},{9,8},{10,11... | collective-permute-start | bytes 3145736 | tf_op jit(solution)/shard_map/ppermute | solution.py:181
  84.2 140.1 %collective-permute-start.4 = (bf16[256,1024]{1,0:T(8,128)(2,1)}, bf16[256,1024]{1,0:T(8,128)(2,1)}, u32[]{:S(2)}, u32[]{:S(2)}) collective-permute-start(bf16[256,1024]{1,0:T(8,128)(2,1)} %collective-permute-done.3), channel_id=1, source_target_pairs={{0,2},{2,0},{4,6},{6,4},{8,10},{10,8},{12,14},{14,12},{16,18},{18,... | collective-permute-start | bytes 1572872 | tf_op jit(solution)/shard_map/ppermute | solution.py:184
  86.4 114.1 %collective-permute-start.2 = (bf16[3,512,512]{2,1,0:T(8,128)(2,1)}, bf16[3,512,512]{2,1,0:T(8,128)(2,1)}, u32[]{:S(2)}, u32[]{:S(2)}) collective-permute-start(bf16[3,512,512]{2,1,0:T(8,128)(2,1)} %collective-permute-done.1), channel_id=1, source_target_pairs={{0,2},{2,0},{4,6},{6,4},{8,10},{10,8},{12,14},{14,12},{16,18},{18,... | collective-permute-start | bytes 4718600 | tf_op jit(solution)/shard_map/ppermute | solution.py:184
  200.0 83.1 %collective-permute-start.8 = (bf16[1024,1024]{1,0:T(8,128)(2,1)}, bf16[1024,1024]{1,0:T(8,128)(2,1)}, u32[]{:S(2)}, u32[]{:S(2)}) collective-permute-start(bf16[1024,1024]{1,0:T(8,128)(2,1)} %collective-permute-done.7), channel_id=1, source_target_pairs={{0,2},{2,0},{4,6},{6,4},{8,10},{10,8},{12,14},{14,12},{16,18},{18,... | collective-permute-start | bytes 6291464 | tf_op jit(solution)/shard_map/ppermute | solution.py:184
  200.0 71.5 %collective-permute-start.6 = (bf16[512,2048]{1,0:T(8,128)(2,1)}, bf16[512,2048]{1,0:T(8,128)(2,1)}, u32[]{:S(2)}, u32[]{:S(2)}) collective-permute-start(bf16[512,2048]{1,0:T(8,128)(2,1)} %collective-permute-done.5), channel_id=1, source_target_pairs={{0,2},{2,0},{4,6},{6,4},{8,10},{10,8},{12,14},{14,12},{16,18},{18,... | collective-permute-start | bytes 6291464 | tf_op jit(solution)/shard_map/ppermute | solution.py:184
  347.4 108.6 %collective-permute-start.25 = (bf16[8,64,2048]{2,1,0:T(8,128)(2,1)}, bf16[8,64,2048]{2,1,0:T(8,128)(2,1)}, u32[]{:S(2)}, u32[]{:S(2)}) collective-permute-start(bf16[8,64,2048]{2,1,0:T(8,128)(2,1)} %dynamic-slice_bitcast_fusion.2), channel_id=1, source_target_pairs={{0,2},{2,0},{4,6},{6,4},{8,10},{10,8},{12,14},{14,12},{16,18},{18,... | collective-permute-start | bytes 6291464 | tf_op jit(solution)/shard_map/ppermute | solution.py:184
  395.1 35.2 %collective-permute-start.19 = (bf16[8,32,1024]{2,1,0:T(8,128)(2,1)}, bf16[8,32,1024]{2,1,0:T(8,128)(2,1)}, u32[]{:S(2)}, u32[]{:S(2)}) collective-permute-start(bf16[8,32,1024]{2,1,0:T(8,128)(2,1)} %dynamic-slice_bitcast_fusion.13), channel_id=1, source_target_pairs={{0,2},{2,0},{4,6},{6,4},{8,10},{10,8},{12,14},{14,12},{16,18},{18,... | collective-permute-start | bytes 1572872 | tf_op jit(solution)/shard_map/ppermute | solution.py:184
  411.2 22.9 %collective-permute-start.13 = (bf16[8,192,512]{2,1,0:T(8,128)(2,1)}, bf16[8,192,512]{2,1,0:T(8,128)(2,1)}, u32[]{:S(2)}, u32[]{:S(2)}) collective-permute-start(bf16[8,192,512]{2,1,0:T(8,128)(2,1)} %dynamic-slice_bitcast_fusion.4), channel_id=1, source_target_pairs={{0,2},{2,0},{4,6},{6,4},{8,10},{10,8},{12,14},{14,12},{16,18},{18,... | collective-permute-start | bytes 4718600 | tf_op jit(solution)/shard_map/ppermute | solution.py:184
  416.2 24.9 %collective-permute-start.18 = (bf16[8,32,1024]{2,1,0:T(8,128)(2,1)}, bf16[8,32,1024]{2,1,0:T(8,128)(2,1)}, u32[]{:S(2)}, u32[]{:S(2)}) collective-permute-start(bf16[8,32,1024]{2,1,0:T(8,128)(2,1)} %dynamic-slice_bitcast_fusion.14), channel_id=1, source_target_pairs={{0,2},{2,0},{4,6},{6,4},{8,10},{10,8},{12,14},{14,12},{16,18},{18,... | collective-permute-start | bytes 1572872 | tf_op jit(solution)/shard_map/ppermute | solution.py:184
  430.2 31.2 %collective-permute-start.12 = (bf16[8,192,512]{2,1,0:T(8,128)(2,1)S(1)}, bf16[8,192,512]{2,1,0:T(8,128)(2,1)S(1)}, u32[]{:S(2)}, u32[]{:S(2)}) collective-permute-start(bf16[8,192,512]{2,1,0:T(8,128)(2,1)S(1)} %dynamic-slice_bitcast_fusion.5), channel_id=1, source_target_pairs={{0,2},{2,0},{4,6},{6,4},{8,10},{10,8},{12,14},{14,12},{16,18},{18,... | collective-permute-start | bytes 4718600 | tf_op jit(solution)/shard_map/ppermute | solution.py:184
  432.3 14.9 %collective-permute-start.20 = (bf16[8,32,1024]{2,1,0:T(8,128)(2,1)S(1)}, bf16[8,32,1024]{2,1,0:T(8,128)(2,1)S(1)}, u32[]{:S(2)}, u32[]{:S(2)}) collective-permute-start(bf16[8,32,1024]{2,1,0:T(8,128)(2,1)S(1)} %fusion.59), channel_id=1, source_target_pairs={{0,1},{1,0},{2,3},{3,2},{4,5},{5,4},{6,7},{7,6},{8,9},{9,8},{10,11... | collective-permute-start | bytes 1572872 | tf_op jit(solution)/shard_map/ppermute | solution.py:181
  436.0 44.9 %collective-permute-start.14 = (bf16[8,192,512]{2,1,0:T(8,128)(2,1)S(1)}, bf16[8,192,512]{2,1,0:T(8,128)(2,1)S(1)}, u32[]{:S(2)}, u32[]{:S(2)}) collective-permute-start(bf16[8,192,512]{2,1,0:T(8,128)(2,1)S(1)} %fusion.42), channel_id=1, source_target_pairs={{0,1},{1,0},{2,3},{3,2},{4,5},{5,4},{6,7},{7,6},{8,9},{9,8},{10,11... | collective-permute-start | bytes 4718600 | tf_op jit(solution)/shard_map/ppermute | solution.py:181
  451.9 66.7 %collective-permute-start.24 = (bf16[8,64,2048]{2,1,0:T(8,128)(2,1)}, bf16[8,64,2048]{2,1,0:T(8,128)(2,1)}, u32[]{:S(2)}, u32[]{:S(2)}) collective-permute-start(bf16[8,64,2048]{2,1,0:T(8,128)(2,1)} %dynamic-slice_bitcast_fusion.3), channel_id=1, source_target_pairs={{0,2},{2,0},{4,6},{6,4},{8,10},{10,8},{12,14},{14,12},{16,18},{18,... | collective-permute-start | bytes 6291464 | tf_op jit(solution)/shard_map/ppermute | solution.py:184
  459.8 65.6 %collective-permute-start.26 = (bf16[8,64,2048]{2,1,0:T(8,128)(2,1)}, bf16[8,64,2048]{2,1,0:T(8,128)(2,1)}, u32[]{:S(2)}, u32[]{:S(2)}) collective-permute-start(bf16[8,64,2048]{2,1,0:T(8,128)(2,1)} %fusion.40), channel_id=1, source_target_pairs={{0,1},{1,0},{2,3},{3,2},{4,5},{5,4},{6,7},{7,6},{8,9},{9,8},{10,11... | collective-permute-start | bytes 6291464 | tf_op jit(solution)/shard_map/ppermute | solution.py:181
  483.6 18.9 %collective-permute-start.15 = (bf16[4,192,512]{2,1,0:T(8,128)(2,1)}, bf16[4,192,512]{2,1,0:T(8,128)(2,1)}, u32[]{:S(2)}, u32[]{:S(2)}) collective-permute-start(bf16[4,192,512]{2,1,0:T(8,128)(2,1)} %dynamic-slice_bitcast_fusion.10), channel_id=1, source_target_pairs={{0,4},{2,6},{4,0},{6,2},{8,12},{10,14},{12,8},{14,10},{16,20},{18,... | collective-permute-start | bytes 2359304 | tf_op jit(solution)/shard_map/ppermute | solution.py:184
  496.4 362.2 %all-gather.9.cloned.1.call-start = ((), (), s32[]{:S(2)}) async-start(), calls=%async_computation | async-start | bytes 3342336 | tf_op jit(solution)/shard_map/all_gather | solution.py:298
  515.4 14.8 %collective-permute-start.17 = (bf16[1,192,512]{2,1,0:T(8,128)(2,1)S(1)}, bf16[1,192,512]{2,1,0:T(8,128)(2,1)S(1)}, u32[]{:S(2)}, u32[]{:S(2)}) collective-permute-start(bf16[1,192,512]{2,1,0:T(8,128)(2,1)S(1)} %constant_dynamic-slice_fusion.4), channel_id=1, source_target_pairs={{0,16},{2,18},{4,20},{6,22},{8,24},{10,26},{12,28},{14,30},{16,0},... | collective-permute-start | bytes 589832 | tf_op jit(solution)/shard_map/ppermute | solution.py:184
  531.0 333.1 %all-gather.13.cloned.1.call-start = ((), (), s32[]{:S(2)}) async-start(), calls=%async_computation.2 | async-start | bytes 4456448 | tf_op jit(solution)/shard_map/all_gather | solution.py:298
  532.5 26.9 %collective-permute-start.27 = (bf16[4,64,2048]{2,1,0:T(8,128)(2,1)S(1)}, bf16[4,64,2048]{2,1,0:T(8,128)(2,1)S(1)}, u32[]{:S(2)}, u32[]{:S(2)}) collective-permute-start(bf16[4,64,2048]{2,1,0:T(8,128)(2,1)S(1)} %dynamic-slice_bitcast_fusion.7), channel_id=1, source_target_pairs={{0,4},{2,6},{4,0},{6,2},{8,12},{10,14},{12,8},{14,10},{16,20},{18,... | collective-permute-start | bytes 3145736 | tf_op jit(solution)/shard_map/ppermute | solution.py:184
  561.1 24.7 %collective-permute-start.28 = (bf16[2,64,2048]{2,1,0:T(8,128)(2,1)S(1)}, bf16[2,64,2048]{2,1,0:T(8,128)(2,1)S(1)}, u32[]{:S(2)}, u32[]{:S(2)}) collective-permute-start(bf16[2,64,2048]{2,1,0:T(8,128)(2,1)S(1)} %dynamic-slice_bitcast_fusion.12), channel_id=1, source_target_pairs={{0,8},{2,10},{4,12},{6,14},{8,0},{10,2},{12,4},{14,6},{16,24},{18,... | collective-permute-start | bytes 1572872 | tf_op jit(solution)/shard_map/ppermute | solution.py:184
  586.0 16.0 %collective-permute-start.29 = (bf16[1,64,2048]{2,1,0:T(8,128)(2,1)S(1)}, bf16[1,64,2048]{2,1,0:T(8,128)(2,1)S(1)}, u32[]{:S(2)}, u32[]{:S(2)}) collective-permute-start(bf16[1,64,2048]{2,1,0:T(8,128)(2,1)S(1)} %constant_dynamic-slice_fusion.2), channel_id=1, source_target_pairs={{0,16},{2,18},{4,20},{6,22},{8,24},{10,26},{12,28},{14,30},{16,0},... | collective-permute-start | bytes 786440 | tf_op jit(solution)/shard_map/ppermute | solution.py:184
  602.8 268.0 %all-gather.15.cloned.1.call-start = ((), (), s32[]{:S(2)}) async-start(), calls=%async_computation.3 | async-start | bytes 4456448 | tf_op jit(solution)/shard_map/all_gather | solution.py:298
  617.8 48.1 %collective-permute-start.32 = (bf16[8,128,1024]{2,1,0:T(8,128)(2,1)S(1)}, bf16[8,128,1024]{2,1,0:T(8,128)(2,1)S(1)}, u32[]{:S(2)}, u32[]{:S(2)}) collective-permute-start(bf16[8,128,1024]{2,1,0:T(8,128)(2,1)S(1)} %fusion.38), channel_id=1, source_target_pairs={{0,1},{1,0},{2,3},{3,2},{4,5},{5,4},{6,7},{7,6},{8,9},{9,8},{10,11... | collective-permute-start | bytes 6291464 | tf_op jit(solution)/shard_map/ppermute | solution.py:181
  667.6 24.8 %collective-permute-start.33 = (bf16[4,128,1024]{2,1,0:T(8,128)(2,1)S(1)}, bf16[4,128,1024]{2,1,0:T(8,128)(2,1)S(1)}, u32[]{:S(2)}, u32[]{:S(2)}) collective-permute-start(bf16[4,128,1024]{2,1,0:T(8,128)(2,1)S(1)} %dynamic-slice_bitcast_fusion.6), channel_id=1, source_target_pairs={{0,4},{2,6},{4,0},{6,2},{8,12},{10,14},{12,8},{14,10},{16,20},{18,... | collective-permute-start | bytes 3145736 | tf_op jit(solution)/shard_map/ppermute | solution.py:184
  722.7 89.0 %collective-permute-start.9 = (bf16[1024,512]{0,1:T(8,128)(2,1)}, bf16[1024,512]{0,1:T(8,128)(2,1)}, u32[]{:S(2)}, u32[]{:S(2)}) collective-permute-start(bf16[1024,512]{0,1:T(8,128)(2,1)} %dynamic-slice_bitcast_fusion.9), channel_id=1, source_target_pairs={{0,1},{1,0},{2,3},{3,2},{4,5},{5,4},{6,7},{7,6},{8,9},{9,8},{10,11... | collective-permute-start | bytes 3145736 | tf_op jit(solution)/shard_map/ppermute | solution.py:181
  754.3 64.5 %collective-permute-start.11 = (bf16[1024,512]{0,1:T(8,128)(2,1)}, bf16[1024,512]{0,1:T(8,128)(2,1)}, u32[]{:S(2)}, u32[]{:S(2)}) collective-permute-start(bf16[1024,512]{0,1:T(8,128)(2,1)} %dynamic-slice_bitcast_fusion.8), channel_id=1, source_target_pairs={{0,1},{1,0},{2,3},{3,2},{4,5},{5,4},{6,7},{7,6},{8,9},{9,8},{10,11... | collective-permute-start | bytes 3145736 | tf_op jit(solution)/shard_map/ppermute | solution.py:181
  (54 other events, 953.3 us)
Sparse Core Ops, SparseCore 0:
  496.6 39.4 all-gather.10
  538.4 52.2 all-gather.8
  602.9 50.5 all-gather.12
  720.5 48.9 all-gather.14

commit v2 on v1

v2 whole, which is shorter than its diff:
```python
from functools import partial

import jax
import jax.numpy as jnp
from jax import lax
from jax.experimental import pallas as pl
from jax.experimental.pallas import tpu as pltpu
from jax.sharding import PartitionSpec as P


HEAD_DIM = 64
F32 = jnp.float32
BF16 = jnp.bfloat16
NT = (((1,), (1,)), ((), ()))
TN = (((0,), (0,)), ((), ()))
NN = (((1,), (0,)), ((), ()))


def dot(a, b, dims=NN, out=F32):
    return lax.dot_general(a, b, dims, preferred_element_type=F32).astype(out)


hold = lax.optimization_barrier


def params(limit=None):
    return pltpu.CompilerParams(dimension_semantics=("arbitrary",), vmem_limit_bytes=limit)


def gather_body(idx_ref, a_ref, *refs):
    idx = idx_ref[0]
    length = a_ref.shape[1]
    hit = lax.broadcasted_iota(jnp.int32, (idx.shape[0], length), 1) == idx
    refs[-1][0] = dot(hit.astype(F32).astype(BF16), a_ref[0], out=BF16)
    if len(refs) > 1:
        seg_ref, doc_ref, _ = refs
        doc_ref[0] = jnp.sum(jnp.where(hit, seg_ref[0], 0), axis=1, keepdims=True)


def gather_rows(source, route_index, segments=None):
    seqs, cap = route_index.shape
    width = source.shape[1]
    length = source.shape[0] // seqs
    column = pl.BlockSpec((1, cap, 1), lambda i: (i, 0, 0))
    in_specs = [column, pl.BlockSpec((1, length, width), lambda i: (i, 0, 0))]
    args = [route_index[:, :, None], source.reshape(seqs, length, width)]
    out_specs = [pl.BlockSpec((1, cap, width), lambda i: (i, 0, 0))]
    out_shape = [jax.ShapeDtypeStruct((seqs, cap, width), BF16)]
    if segments is not None:
        in_specs.append(pl.BlockSpec((1, 1, length), lambda i: (i, 0, 0)))
        args.append(segments.reshape(seqs, 1, length))
        out_specs.insert(0, column)
        out_shape.insert(0, jax.ShapeDtypeStruct((seqs, cap, 1), jnp.int32))
    return pl.pallas_call(
        gather_body,
        grid=(seqs,),
        in_specs=in_specs,
        out_specs=out_specs,
        out_shape=out_shape,
        compiler_params=params(),
        name="gather_rows",
    )(*args)


def scatter_body(idx_ref, new_ref, a_ref, out_ref):
    idx = idx_ref[0]
    length = a_ref.shape[1]
    hit = lax.broadcasted_iota(jnp.int32, (length, idx.shape[1]), 0) == idx
    place = hit.astype(F32)
    routed = jnp.max(place, axis=1, keepdims=True) > 0.5
    moved = dot(place.astype(BF16), new_ref[0])
    out_ref[0] = jnp.where(routed, moved, a_ref[0].astype(F32)).astype(BF16)


def scatter_rows(base, rows, route_index):
    seqs, cap = route_index.shape
    width = base.shape[1]
    length = base.shape[0] // seqs
    big = pl.BlockSpec((1, length, width), lambda i: (i, 0, 0))
    out = pl.pallas_call(
        scatter_body,
        grid=(seqs,),
        in_specs=[
            pl.BlockSpec((1, 1, cap), lambda i: (i, 0, 0)),
            pl.BlockSpec((1, cap, width), lambda i: (i, 0, 0)),
            big,
        ],
        out_specs=big,
        out_shape=jax.ShapeDtypeStruct((seqs, length, width), BF16),
        compiler_params=params(),
        name="scatter_rows",
    )(route_index[:, None, :], rows, base.reshape(seqs, length, width))
    return out.reshape(base.shape)


def probs_of(query, key, allowed):
    scores = dot(key, query * HEAD_DIM ** (-0.5), NT)
    scores = jnp.where(allowed, scores, -1e30)
    expo = jnp.exp(scores - jnp.max(scores, axis=0, keepdims=True))
    return expo * (1.0 / jnp.sum(expo, axis=0, keepdims=True))


def allowed_of(pos_c, pos_r, doc_c, doc_r):
    return (pos_c[0] <= pos_r[0]) & (doc_r[0] == doc_c[0])


def head_groups(width):
    heads = range(width // HEAD_DIM)
    return [heads[i : i + 2] for i in range(0, len(heads), 2)]


def columns(head, count=1):
    return slice(head * HEAD_DIM, (head + count) * HEAD_DIM)


def attend_body(pos_c, pos_r, doc_c, doc_r, qkv_ref, out_ref):
    allowed = allowed_of(pos_c, pos_r, doc_c, doc_r)
    for group in head_groups(qkv_ref.shape[2]):
        turned = []
        for head in group:
            cols = columns(head)
            probs = probs_of(qkv_ref[0, :, cols], qkv_ref[1, :, cols], allowed)
            turned.append(dot(qkv_ref[2, :, cols], probs.astype(BF16), TN))
        out_ref[:, columns(group[0], len(group))] = jnp.concatenate(turned, 0).T.astype(BF16)


def attend_back_body(pos_c, pos_r, doc_c, doc_r, qkv_ref, grad_ref, out_ref):
    allowed = allowed_of(pos_c, pos_r, doc_c, doc_r)
    scale = HEAD_DIM ** (-0.5)
    for group in head_groups(qkv_ref.shape[2]):
        turned = []
        for head in group:
            cols = columns(head)
            query, key, value = (qkv_ref[c, :, cols] for c in range(3))
            grad = grad_ref[:, cols]
            probs = probs_of(query, key, allowed)
            prob_grad = dot(value, grad, NT)
            row_dot = jnp.sum(probs * prob_grad, axis=0, keepdims=True)
            score_grad = (probs * (prob_grad - row_dot)).astype(BF16)
            turned.append(dot(key, score_grad, TN))
            out_ref[1, :, cols] = (dot(score_grad, query) * scale).astype(BF16)
            out_ref[2, :, cols] = dot(probs.astype(BF16), grad, out=BF16)
        both = jnp.concatenate(turned, 0).T * scale
        out_ref[0, :, columns(group[0], len(group))] = both.astype(BF16)


def attention(body, masks, cap, qkv, *more):
    width = qkv.shape[2]
    seqs = qkv.shape[1] // cap
    column = pl.BlockSpec((1, cap, 1), lambda i: (i, 0, 0))
    line = pl.BlockSpec((1, 1, cap), lambda i: (i, 0, 0))
    three = pl.BlockSpec((3, cap, width), lambda i: (0, i, 0))
    one = pl.BlockSpec((cap, width), lambda i: (i, 0))
    back = bool(more)
    return pl.pallas_call(
        body,
        grid=(seqs,),
        in_specs=[column, line, column, line, three] + [one] * len(more),
        out_specs=three if back else one,
        out_shape=jax.ShapeDtypeStruct(qkv.shape if back else qkv.shape[1:], BF16),
        compiler_params=params(),
        name="attend_back" if back else "attend",
    )(*masks, qkv, *more)


def gelu_parts(v):
    c = 0.7978845608028654
    th = jnp.tanh(c * (v + 0.044715 * (v * v * v)))
    half = 0.5 * (1.0 + th)
    slope = half + 0.5 * v * (1.0 - th * th) * (c * (1.0 + 3 * 0.044715 * (v * v)))
    return v * half, slope


def shards(
    sizes,
    layer_in,
    out_grad,
    route_index,
    segments,
    w_project,
    w_output,
    w_expand,
    w_reduce,
    gain_first,
    gain_second,
    w_router,
):
    copies, parts = sizes
    seq_local, cap = route_index.shape
    width = layer_in.shape[1]
    full = gain_first.shape[0]
    own_seqs = seq_local // parts
    own_rows = own_seqs * cap
    here = lax.axis_index("tensor")
    place = lax.axis_index("dp")
    core = place & 1

    def shift_plain(value, step):
        return lax.ppermute(value, "tensor", [(s, (s + step) % parts) for s in range(parts)])

    def flip_plain(value, bit):
        return lax.ppermute(value, "dp", [(s, s ^ bit) for s in range(copies)])

    def ordered(pieces):
        stacked = jnp.stack(pieces)
        if parts == 2:
            return [
                jnp.where(here == 0, pieces[0], pieces[1]),
                jnp.where(here == 0, pieces[1], pieces[0]),
            ]
        return [
            lax.dynamic_index_in_dim(stacked, (here - s) % parts, keepdims=False)
            for s in range(parts)
        ]

    def group_at(value, index):
        return lax.dynamic_index_in_dim(value, index % parts, keepdims=False)

    def to_rows(local):
        grouped = local.reshape(parts, own_rows, width)
        pieces = [group_at(grouped, here)]
        for k in range(1, parts):
            pieces.append(shift_plain(group_at(grouped, here + k), k))
        return jnp.concatenate(ordered(pieces), axis=1)

    def to_features(value):
        blocks = value.reshape(own_rows, parts, width).transpose(1, 0, 2)
        pieces = [group_at(blocks, here)]
        for k in range(1, parts):
            pieces.append(shift_plain(group_at(blocks, here + k), k))
        return jnp.concatenate(ordered(pieces), axis=0).reshape(seq_local, cap, width)

    def far(weight, k, axis):
        half = weight.shape[axis] // 2
        mine = lax.dynamic_slice_in_dim(weight, core * half, half, axis)
        mine = shift_plain(mine, -k)
        other = flip_plain(mine, 1)
        return jnp.where(
            core == 0,
            jnp.concatenate([mine, other], axis),
            jnp.concatenate([other, mine], axis),
        )

    def spread(weight, k):
        step = weight.shape[0] // copies
        return shift_plain(lax.dynamic_slice_in_dim(weight, place * step, step, 0), -k)

    slices = [(spread(w_expand, k), spread(w_reduce, k)) for k in range(1, parts)]
    docs, rows_local = gather_rows(layer_in, route_index, segments)
    rows_local, slices = hold((rows_local, slices))
    gathered = lax.all_gather(slices, "dp", axis=0, tiled=True)
    expand_all = [w_expand] + [pair[0] for pair in gathered]
    reduce_all = [w_reduce] + [pair[1] for pair in gathered]
    rows_in = to_rows(rows_local)
    (cot_local,) = gather_rows(out_grad, route_index)
    rows_in, cot_local, w_project_late, w_output_late = hold(
        (rows_in, cot_local, w_project, w_output)
    )
    project_far = [far(w_project_late, k, 1) for k in range(1, parts)]
    output_far = [far(w_output_late, k, 0) for k in range(1, parts)]
    cot_local, project_far = hold((cot_local, project_far))
    cot_in = to_rows(cot_local)
    project_all = [w_project] + project_far
    output_all = [w_output] + output_far
    rows = rows_in.astype(F32)
    cot = cot_in.astype(F32)
    positions = group_at(route_index.reshape(parts, own_seqs, cap), here)
    docs = group_at(docs.reshape(parts, own_seqs, cap), here)
    masks = (positions[:, :, None], positions[:, None, :], docs[:, :, None], docs[:, None, :])
    gain_one = gain_first.astype(F32)
    gain_two = gain_second.astype(F32)
    router_row = w_router.astype(F32)

    router = jnp.sum(rows * router_row, axis=1, keepdims=True)
    scale_first = lax.rsqrt(jnp.mean(rows * rows, axis=1, keepdims=True) + 1e-06)
    normed = (rows * scale_first * gain_one).astype(BF16)

    def heads_of(w):
        qkv = jnp.einsum("rd,cde->cre", normed, w, preferred_element_type=F32).astype(BF16)
        return qkv, attention(attend_body, masks, cap, qkv)

    heads_all = [heads_of(w_project)]
    heads_all += [heads_of(w) for w in project_far]
    qkv_all = [pair[0] for pair in heads_all]
    attended_all = [pair[1] for pair in heads_all]
    attn_out = sum(dot(a, w) for a, w in zip(attended_all, output_all))
    hidden = rows + attn_out
    scale_second = lax.rsqrt(jnp.mean(hidden * hidden, axis=1, keepdims=True) + 1e-06)
    normed_two = (hidden * scale_second * gain_two).astype(BF16)
    mixer_grad = (router * cot).astype(BF16)
    activated_all = []
    slope_all = []
    for w in expand_all:
        act, slope = gelu_parts(dot(normed_two, w))
        activated_all.append(act.astype(BF16))
        slope_all.append(slope.astype(BF16))

    def add(a, b):
        return (a.astype(F32) + b.astype(F32)).astype(BF16)

    def blocks_of(grads):
        return [g.reshape((copies, g.shape[0] // copies) + g.shape[1:]) for g in grads]

    def send(values, bit):
        lead = values[0].shape[0] // 2
        pairs = [v.reshape((lead, 2) + v.shape[1:]) for v in values]
        index = (place // bit) & 1
        kept = [lax.dynamic_index_in_dim(v, index, 1, keepdims=False) for v in pairs]
        away = [lax.dynamic_index_in_dim(v, 1 - index, 1, keepdims=False) for v in pairs]
        return kept, [flip_plain(v, bit) for v in away]

    def merge(sent):
        return [add(a, b) for a, b in zip(*sent)]

    def cross(values):
        return values[:1], [shift_plain(values[k], k) for k in range(1, parts)]

    def merge_cross(sent):
        total = sent[0][0]
        for other in sent[1]:
            total = add(total, other)
        return [total]

    def finish(values, bit):
        while bit < copies:
            values = merge(send(values, bit))
            bit *= 2
        return values[0].reshape(values[0].shape[1:])

    reduce_grads = [dot(a, mixer_grad, TN, BF16) for a in activated_all]
    reduce_grads, mixer_grad, slope_all = hold((reduce_grads, mixer_grad, slope_all))
    sent_r = send(blocks_of(reduce_grads), 1)
    back_all = [
        (dot(mixer_grad, w, NT) * slope.astype(F32)).astype(BF16)
        for w, slope in zip(reduce_all, slope_all)
    ]
    back_all, part_r = hold((back_all, merge(sent_r)))
    sent_r = cross(part_r)
    expand_grads = [dot(normed_two, g, TN, BF16) for g in back_all]
    expand_grads, back_all, activated_all = hold((expand_grads, back_all, activated_all))
    sent_e = send(blocks_of(expand_grads), 1)
    mixer_out = sum(dot(a, w) for a, w in zip(activated_all, reduce_all))
    branch = attn_out + mixer_out
    layer_rows = (rows + router * branch).astype(BF16)
    router_grad = jnp.sum(cot * branch, axis=1, keepdims=True)
    layer_rows, router_grad, back_all, part_e, part_r = hold(
        (layer_rows, router_grad, back_all, merge(sent_e), merge_cross(sent_r))
    )
    sent_r = send(part_r, 2)
    sent_e = cross(part_e)
    two_grad = sum(dot(g, w, NT) for g, w in zip(back_all, expand_all))
    hidden_hat = hidden * scale_second
    weighted_two = two_grad * gain_two
    gain_two_part = jnp.sum(two_grad * hidden_hat, axis=0)
    stat_two = jnp.mean(weighted_two * hidden_hat, axis=1, keepdims=True)
    hidden_grad = scale_second * (weighted_two - hidden_hat * stat_two)
    branch_grad = (router * cot + hidden_grad).astype(BF16)
    branch_parts = branch_grad.reshape(own_rows, parts, width)
    output_grads = [
        jnp.einsum("re,rcd->ced", a, branch_parts, preferred_element_type=F32)
        .astype(BF16)
        .reshape(full, width)
        for a in attended_all
    ]
    back_heads = [dot(branch_grad, w, NT, BF16) for w in output_all]
    back_heads, output_grads, part_r = hold((back_heads, output_grads, merge(sent_r)))
    sent_r = send(part_r, 4)
    sent_o = send(blocks_of(output_grads), 1)

    def heads_back(k):
        return attention(attend_back_body, masks, cap, qkv_all[k], back_heads[k])

    def weight_grad(back):
        grad = jnp.einsum("rd,cre->cde", normed, back, preferred_element_type=F32)
        return grad.astype(BF16).reshape(3 * full, -1)

    back_far = [heads_back(k) for k in range(1, parts)]
    back_far, part_r, part_e, part_o, layer_rows = hold(
        (back_far, merge(sent_r), merge_cross(sent_e), merge(sent_o), layer_rows)
    )
    sent_e = send(part_e, 2)
    sent_o = cross(part_o)
    layer_moved = to_features(layer_rows)
    sum_r = finish(part_r, 8)
    grads_far = [weight_grad(g) for g in back_far]
    grads_far, sum_r, qkv_all = hold((grads_far, sum_r, qkv_all))
    grad_reduce = lax.all_gather(sum_r, "dp", axis=0, tiled=True)
    sent_p = send(blocks_of(grads_far), 1)
    back_own = heads_back(0)
    back_own, part_e, far_p, part_o = hold(
        (back_own, merge(sent_e), merge(sent_p), merge_cross(sent_o))
    )
    sent_e = send(part_e, 4)
    sent_o = send(part_o, 2)
    moved_p = [shift_plain(g, k + 1) for k, g in enumerate(far_p)]
    grad_own = weight_grad(back_own)
    project_back = [back_own] + back_far
    grad_own, project_back, part_e, part_o = hold(
        (grad_own, project_back, merge(sent_e), merge(sent_o))
    )
    sent_o = send(part_o, 4)
    sum_e = finish(part_e, 8)
    own_p = merge(send(blocks_of([grad_own]), 1))
    normed_grad = sum(
        dot(g[c], w[c], NT) for g, w in zip(project_back, project_all) for c in range(3)
    )
    normed_grad, sum_e, part_o = hold((normed_grad, sum_e, merge(sent_o)))
    grad_expand = lax.all_gather(sum_e, "dp", axis=0, tiled=True)
    rows_hat = rows * scale_first
    weighted_one = normed_grad * gain_one
    gain_one_part = jnp.sum(normed_grad * rows_hat, axis=0)
    stat_one = jnp.mean(weighted_one * rows_hat, axis=1, keepdims=True)
    first_grad = scale_first * (weighted_one - rows_hat * stat_one)
    rows_grad = cot + hidden_grad + first_grad + router_grad * router_row
    router_part = jnp.sum(router_grad * rows, axis=0)
    small = jnp.stack([gain_one_part, gain_two_part, router_part])
    rows_grad, part_p, small, layer_moved = hold(
        (rows_grad.astype(BF16), merge_cross((own_p, moved_p)), small, layer_moved)
    )
    sent_p = send(part_p, 2)
    rows_moved = to_features(rows_grad)
    sum_o = finish(part_o, 8)
    bit = 1
    while bit < copies:
        small = small + flip_plain(small, bit)
        bit *= 2
    total = small
    for k in range(1, parts):
        total = total + shift_plain(small, k)
    small = lax.dynamic_slice_in_dim(total, here * width, width, 1)
    layer_out = scatter_rows(layer_in, layer_moved, route_index)
    layer_out, part_p, rows_moved, sum_o = hold((layer_out, merge(sent_p), rows_moved, sum_o))
    sent_p = send(part_p, 4)
    input_grad = scatter_rows(out_grad, rows_moved, route_index)
    sum_p = finish(merge(sent_p), 8)
    lead = sum_p.shape[0]
    both = jnp.concatenate([sum_p, sum_o], axis=0)
    both, grad_reduce, grad_expand = hold((both, grad_reduce, grad_expand))
    both = lax.all_gather(both, "dp", axis=0)
    grad_project = both[:, :lead].astype(F32).reshape(3, full, width)
    output_sum = both[:, lead:].reshape(parts, width, width).transpose(1, 0, 2)
    output_sum = output_sum.reshape(width, full)
    grad_reduce = grad_reduce.astype(F32)
    grad_expand = grad_expand.astype(F32)
    output_sum = output_sum.astype(F32)
    return (
        layer_out,
        input_grad,
        grad_project,
        output_sum,
        grad_expand,
        grad_reduce,
        small[0],
        small[1],
        small[2],
    )


def labelled(sizes, *args):
    return shards(sizes, *args)


def solution(mesh):
    return jax.shard_map(
        partial(labelled, (mesh.shape["dp"], mesh.shape["tensor"])),
        mesh=mesh,
        in_specs=(
            P("dp", "tensor"),
            P("dp", "tensor"),
            P("dp", None),
            P("dp"),
            P(None, None, "tensor"),
            P("tensor", None),
            P(None, "tensor"),
            P("tensor", None),
            P(),
            P(),
            P(),
        ),
        out_specs=(
            P("dp", "tensor"),
            P("dp", "tensor"),
            P(None, None, "tensor"),
            P("tensor", None),
            P(None, "tensor"),
            P("tensor", None),
            P("tensor"),
            P("tensor"),
            P("tensor"),
        ),
        check_vma=False,
    )
```

time: 894 us -> 662 us (0.74)
  waiting for transfers between devices: 310 us -> 160 us
  blocking collectives: 55 us -> 0 us
  matrix products: 197 us -> 153 us
  other arithmetic: 70.8 us -> 95.2 us
    ppermute x36 -> x39, waiting for transfers between devices: 310 us -> 159 us  [the longest x13 106 us: shift_plain(): lax.ppermute(value, 'tensor', [(s, (s + step) % parts) for s in range(par...]
    psum x1 -> x0, blocking collectives: 55 us -> none  [shards(): lax.psum(jnp.stack([gain_one_part, gain_two_part, router_part]), ('dp', '...]
    dot_general x24 -> x22, matrix products: 172 us -> 127 us  [dot(): return lax.dot_general(a, b, dims, preferred_element_type=F32).astype(out)]
    convert_element_type x20 -> x19, other arithmetic: 25.5 us -> 45.1 us  [add(): return (a.astype(F32) + b.astype(F32)).astype(BF16)]
    pallas_call x4, Pallas kernels: 69.5 us -> 59.5 us  [attention(): pl.pallas_call(body, grid=(seqs,), in_specs=[column, line, column, line,...]
    ppermute x36 -> x39, starting transfers between devices: 43.2 us -> 35.7 us  [the longest x13 18 us: shift_plain(): lax.ppermute(value, 'tensor', [(s, (s + step) % parts) for s in range(par...]
    pallas_call x1 -> x2, Pallas kernels: 19 us -> 25.2 us  [gather_rows(): pl.pallas_call(gather_body, grid=(seqs,), in_specs=in_specs, out_specs=ou...]
    dot_general x4 -> x6, matrix products: 25.4 us -> 26.2 us  [the longest x2 12.6 us: heads_of(): jnp.einsum('rd,cde->cre', normed, w, preferred_element_type=F32)]
  transfers between devices with their start and end apart: 40 -> 44, of which waited for: 16 -> 19; matrix products, arithmetic and copies ran while one was open for 29% -> 44% of each run, Pallas kernels for 14% -> 18%
where the time goes in v2:
time: 662 us; the launch traced here: 656 us
  waiting for transfers between devices  160 us (24%)
  matrix products  153 us (23%)
  Pallas kernels  118 us (18%)
  other arithmetic  95.2 us (14%)
  local copies, waits for them, and re-layouts  78.3 us (12%)
  starting transfers between devices  35.9 us (5%)
  between operations  15.2 us (2%)
    dot_general x22, matrix products, dot(): return lax.dot_general(a, b, dims, preferred_element_type=F32).astype(out)  127 us
    ppermute x13, waiting for transfers between devices, shift_plain(): lax.ppermute(value, 'tensor', [(s, (s + step) % parts) for s in range(par...  106 us
    pallas_call x4, Pallas kernels, attention(): pl.pallas_call(body, grid=(seqs,), in_specs=[column, line, column, line,...  59.5 us
    ppermute x26, waiting for transfers between devices, flip_plain(): return lax.ppermute(value, 'dp', [(s, s ^ bit) for s in range(copies)])  52.8 us
    convert_element_type x19, other arithmetic, add(): return (a.astype(F32) + b.astype(F32)).astype(BF16)  45.1 us
    pallas_call x2, Pallas kernels, scatter_rows(): pl.pallas_call(scatter_body, grid=(seqs,), in_specs=[pl.BlockSpec((1, 1,...  33.3 us
    pallas_call x2, Pallas kernels, gather_rows(): pl.pallas_call(gather_body, grid=(seqs,), in_specs=in_specs, out_specs=ou...  25.2 us
    squeeze x20, local copies, waits for them, and re-layouts, send(): lax.dynamic_index_in_dim(v, 1 - index, 1, keepdims=False)  19.5 us
  transfers between devices with their start and end apart: 44, of which 19 were waited for; matrix products, arithmetic and copies ran while one was open for 44% of the time, Pallas kernels for 18%

profile of v2, /device:TPU:0, one launch (start us, length us, event | category | flops | bytes accessed | tf_op | source)
XLA Modules:
  0.0 655.7 jit_solution(1194015073942458700)
XLA Ops:
  14.4 13.2 %gather_rows.2 = (s32[8,256,1]{2,1,0:T(8,128)}, bf16[8,256,512]{2,1,0:T(8,128)(2,1)}) custom-call(s32[8,256,1]{2,1,0:T(8,128)} %copy.134.idx_ref, bf16[8,2048,512]{2,1,0:T(8,128)(2,1)} %bitcast.274, s32[8,1,2048]{2,1,0:T(1,128)} %bitcast.328), custom_call_target="tpu_custom_call" | custom-call | tf_op jit(solution)/shard_map/gather_rows/pallas_call | solution.py:54
  33.5 11.9 %gather_rows.3 = bf16[8,256,512]{2,1,0:T(8,128)(2,1)} custom-call(s32[8,256,1]{2,1,0:T(8,128)} %copy.134.idx_ref, bf16[8,2048,512]{2,1,0:T(8,128)(2,1)} %bitcast.272), custom_call_target="tpu_custom_call" | custom-call | tf_op jit(solution)/shard_map/gather_rows/pallas_call | solution.py:54
  46.0 10.4 %collective-permute-done.2 = bf16[1024,512]{0,1:T(8,128)(2,1)} collective-permute-done((bf16[1024,512]{0,1:T(8,128)(2,1)}, bf16[1024,512]{0,1:T(8,128)(2,1)}, u32[]{:S(2)}, u32[]{:S(2)}) %collective-permute-start.2) | collective-permute-done | bytes 1048608 | tf_op jit(solution)/shard_map/ppermute | solution.py:199
  67.4 29.7 %collective-permute-done.3 = bf16[3,512,512]{2,1,0:T(8,128)(2,1)} collective-permute-done((bf16[3,512,512]{2,1,0:T(8,128)(2,1)}, bf16[3,512,512]{2,1,0:T(8,128)(2,1)}, u32[]{:S(2)}, u32[]{:S(2)}) %collective-permute-start.3) | collective-permute-done | bytes 1572896 | tf_op jit(solution)/shard_map/ppermute | solution.py:199
  97.6 7.4 %convert_bitcast_fusion.3.qkv_ref = bf16[3,1024,512]{2,1,0:T(8,128)(2,1)} fusion(bf16[3,1024,512]{2,1,0:T(8,128)(2,1)} %param.15, bf16[1024,1024]{0,1:T(8,128)(2,1)S(1)} %pad_maximum_fusion, f32[1024]{0:T(1024)S(1)} %convert_element_type.402, f32[1024]{0:T(1024)S(1)} %add_rsqrt_fusion.1), kind=kOutput, calls=%fused_computation.87 | convolution fusion | flops 3226992640 | bytes 8396800 | tf_op jit(solution)/shard_map/rd,cde->cre/dot_general | solution.py:279
  105.1 13.6 %attend.2 = bf16[1024,512]{1,0:T(8,128)(2,1)} custom-call(s32[4,256,1]{2,1,0:T(8,128)} %copy.141.pos_c, s32[4,1,256]{2,1,0:T(1,128)} %broadcast_in_dim.17.pos_r, s32[4,256,1]{2,1,0:T(8,128)} %copy.142.doc_c, s32[4,1,256]{2,1,0:T(1,128)} %broadcast_in_dim.19.doc_r, bf16[3,1024,512]{2,1,0:T(8,128)(2,1)} %convert_bitcast_fusion.3.qkv_ref), custom_call_target="tpu_custom_call" | custom-call | tf_op jit(solution)/shard_map/attend/pallas_call | solution.py:155
  134.0 13.6 %attend.3 = bf16[1024,512]{1,0:T(8,128)(2,1)} custom-call(s32[4,256,1]{2,1,0:T(8,128)} %copy.141.pos_c, s32[4,1,256]{2,1,0:T(1,128)} %broadcast_in_dim.17.pos_r, s32[4,256,1]{2,1,0:T(8,128)} %copy.142.doc_c, s32[4,1,256]{2,1,0:T(1,128)} %broadcast_in_dim.19.doc_r, bf16[3,1024,512]{2,1,0:T(8,128)(2,1)} %convert_bitcast_fusion.2.qkv_ref), custom_call_target="tpu_custom_call" | custom-call | tf_op jit(solution)/shard_map/attend/pallas_call | solution.py:155
  147.6 7.3 %multiply_reduce_fusion.2 = (f32[1024]{0:T(1024)S(1)}, f32[1024]{0:T(1024)S(1)}, f32[1024,1024]{0,1:T(8,128)}) fusion(bf16[1024,1024]{0,1:T(8,128)(2,1)S(1)} %pad_maximum_fusion, f32[1024]{0:T(1024)S(1)} %convert_element_type.408, f32[1024,1024]{0,1:T(8,128)} %fusion.98, bf16[1024,512]{1,0:T(8,128)(2,1)} %attend.3, ...), kind=kOutput, calls=%fused_computation.73 | convolution fusion | flops 1085798400 | bytes 12595201 | tf_op jit(solution)/shard_map/dot_general | solution.py:20
  166.2 10.7 %fusion.8 = (bf16[1024,2048]{1,0:T(8,128)(2,1)}, bf16[1024,2048]{1,0:T(8,128)(2,1)S(1)}) fusion(bf16[1024,1024]{0,1:T(8,128)(2,1)S(1)} %multiply_convert_fusion.4, bf16[1024,2048]{1,0:T(8,128)(2,1)S(1)} %copy-done.59), kind=kOutput, calls=%fused_computation.18 | convolution fusion | flops 4334813184 | bytes 14680064 | tf_op jit(solution)/shard_map/dot_general | solution.py:20
  176.9 7.1 %collective-permute-done.5 = bf16[1024,512]{0,1:T(8,128)(2,1)} collective-permute-done((bf16[1024,512]{0,1:T(8,128)(2,1)}, bf16[1024,512]{0,1:T(8,128)(2,1)}, u32[]{:S(2)}, u32[]{:S(2)}) %collective-permute-start.5) | collective-permute-done | bytes 1048608 | tf_op jit(solution)/shard_map/ppermute | solution.py:199
  188.5 6.4 convolution_convert_fusion.3
  194.9 13.2 %fusion.17 = (bf16[1024,2048]{1,0:T(8,128)(2,1)}, bf16[1024,2048]{1,0:T(8,128)(2,1)S(1)}) fusion(bf16[1024,1024]{0,1:T(8,128)(2,1)} %copy-done.34, bf16[1024,2048]{1,0:T(8,128)(2,1)} %all-gather.7.cloned.1.call-done), kind=kOutput, calls=%fused_computation.27 | convolution fusion | flops 4334813184 | bytes 14680064 | tf_op jit(solution)/shard_map/dot_general | solution.py:20
  219.2 6.6 %multiply_convert_fusion.1 = bf16[1024,2048]{1,0:T(8,128)(2,1)} fusion(bf16[1024,2048]{1,0:T(8,128)(2,1)S(1)} %copy-done.69, bf16[1024,1024]{0,1:T(8,128)(2,1)S(1)} %copy-done.37, bf16[2048,1024]{1,0:T(8,128)(2,1)S(1)} %copy-done.57), kind=kOutput, calls=%fused_computation.29 | convolution fusion | flops 4301258752 | bytes 14680064 | tf_op jit(solution)/shard_map/dot_general | solution.py:20
  225.8 8.8 %multiply_convert_fusion = bf16[1024,2048]{1,0:T(8,128)(2,1)S(1)} fusion(bf16[1024,2048]{1,0:T(8,128)(2,1)} %get-tuple-element.92, bf16[1024,1024]{0,1:T(8,128)(2,1)} %copy-done.36, bf16[2048,1024]{1,0:T(8,128)(2,1)} %all-gather.9.cloned.1.call-done), kind=kOutput, calls=%fused_computation.28 | convolution fusion | flops 4301258752 | bytes 14680064 | tf_op jit(solution)/shard_map/dot_general | solution.py:20
  261.7 6.3 fusion.99
  268.0 12.4 %fusion.25 = (f32[1024]{0:T(1024)}, bf16[1024,1024]{0,1:T(8,128)(2,1)}) fusion(bf16[1024,512]{0,1:T(8,128)(2,1)S(1)} %copy-done.8, bf16[1024,512]{0,1:T(8,128)(2,1)S(1)} %copy-done.5, f32[1024]{0:T(1024)S(1)} %get-tuple-element.173, bf16[1024,1024]{0,1:T(8,128)(2,1)S(1)} %pad_maximum_fusion, f32[1024,1024]{0,1:T(8,128)S(1)} %copy-done.1, ...), kind=kOutput, calls=%fused_computation.44 | convolution fusion | flops 4307549184 | bytes 23076864 | tf_op jit(solution)/shard_map/dot_general | solution.py:20
  296.9 6.5 fusion.100
  303.4 9.1 %multiply_reduce_fusion = (f32[1024]{0:T(1024)}, f32[1024]{0:T(1024)S(1)}, f32[1024,1024]{0,1:T(8,128)S(1)}) fusion(f32[1024]{0:T(1024)S(1)} %add_rsqrt_fusion, f32[1024,1024]{0,1:T(8,128)S(1)} %copy-done.1, bf16[1024,1024]{0,1:T(8,128)(2,1)S(1)} %pad_maximum_fusion, f32[1024]{0:T(1024)S(1)} %convert_element_type.409, f32[1024,1024]{0,1:T(8,128)} %fusion.100, ...), kind=kOutput, calls=%fused_computation.65 | convolution fusion | flops 4304402432 | bytes 23085056 | tf_op jit(solution)/shard_map/dot_general | solution.py:20
  334.5 16.1 %attend_back.2 = bf16[3,1024,512]{2,1,0:T(8,128)(2,1)} custom-call(s32[4,256,1]{2,1,0:T(8,128)} %copy.141.pos_c, s32[4,1,256]{2,1,0:T(1,128)} %broadcast_in_dim.17.pos_r, s32[4,256,1]{2,1,0:T(8,128)} %copy.142.doc_c, s32[4,1,256]{2,1,0:T(1,128)} %broadcast_in_dim.19.doc_r, bf16[3,1024,512]{2,1,0:T(8,128)(2,1)} %convert_bitcast_fusion.2.qkv_ref, ...), custom_call_target="tpu_custom_call" | custom-call | tf_op jit(solution)/shard_map/attend_back/pallas_call | solution.py:155
  356.8 8.8 %collective-permute-done.15 = bf16[8,64,2048]{2,1,0:T(8,128)(2,1)} collective-permute-done((bf16[8,64,2048]{2,1,0:T(8,128)(2,1)}, bf16[8,64,2048]{2,1,0:T(8,128)(2,1)}, u32[]{:S(2)}, u32[]{:S(2)}) %collective-permute-start.15) | collective-permute-done | bytes 2097184 | tf_op jit(solution)/shard_map/ppermute | solution.py:199
  371.8 5.6 convert_bitcast_fusion.1
  391.4 16.1 %attend_back.3 = bf16[3,1024,512]{2,1,0:T(8,128)(2,1)} custom-call(s32[4,256,1]{2,1,0:T(8,128)} %copy.141.pos_c, s32[4,1,256]{2,1,0:T(1,128)} %broadcast_in_dim.17.pos_r, s32[4,256,1]{2,1,0:T(8,128)} %copy.142.doc_c, s32[4,1,256]{2,1,0:T(1,128)} %broadcast_in_dim.19.doc_r, bf16[3,1024,512]{2,1,0:T(8,128)(2,1)} %convert_bitcast_fusion.3.qkv_ref, ...), custom_call_target="tpu_custom_call" | custom-call | tf_op jit(solution)/shard_map/attend_back/pallas_call | solution.py:155
  409.0 9.1 %collective-permute-done.19 = bf16[4,64,2048]{2,1,0:T(8,128)(2,1)} collective-permute-done((bf16[4,64,2048]{2,1,0:T(8,128)(2,1)}, bf16[4,64,2048]{2,1,0:T(8,128)(2,1)}, u32[]{:S(2)}, u32[]{:S(2)}) %collective-permute-start.19) | collective-permute-done | bytes 1048608 | tf_op jit(solution)/shard_map/ppermute | solution.py:202
  437.5 9.4 %collective-permute-done.22 = bf16[2,64,2048]{2,1,0:T(8,128)(2,1)} collective-permute-done((bf16[2,64,2048]{2,1,0:T(8,128)(2,1)}, bf16[2,64,2048]{2,1,0:T(8,128)(2,1)}, u32[]{:S(2)}, u32[]{:S(2)}) %collective-permute-start.22) | collective-permute-done | bytes 524320 | tf_op jit(solution)/shard_map/ppermute | solution.py:202
  470.7 22.2 %collective-permute-done.28 = bf16[1024,512]{0,1:T(8,128)(2,1)S(1)} collective-permute-done((bf16[1024,512]{0,1:T(8,128)(2,1)S(1)}, bf16[1024,512]{0,1:T(8,128)(2,1)S(1)}, u32[]{:S(2)}, u32[]{:S(2)}) %collective-permute-start.28) | collective-permute-done | bytes 1048608 | tf_op jit(solution)/shard_map/ppermute | solution.py:199
  513.3 20.9 %collective-permute-done.27 = bf16[8,192,512]{2,1,0:T(8,128)(2,1)S(1)} collective-permute-done((bf16[8,192,512]{2,1,0:T(8,128)(2,1)}, bf16[8,192,512]{2,1,0:T(8,128)(2,1)S(1)}, u32[]{:S(2)}, u32[]{:S(2)}) %collective-permute-start.27) | collective-permute-done | bytes 1572896 | tf_op jit(solution)/shard_map/ppermute | solution.py:199
  545.1 16.6 %scatter_rows.2 = bf16[8,2048,512]{2,1,0:T(8,128)(2,1)} custom-call(s32[8,1,256]{2,1,0:T(1,128)} %broadcast_in_dim.14.idx_ref, bf16[8,256,512]{2,1,0:T(8,128)(2,1)} %bitcast.287, bf16[8,2048,512]{2,1,0:T(8,128)(2,1)} %bitcast.275), custom_call_target="tpu_custom_call" | custom-call | tf_op jit(solution)/shard_map/scatter_rows/pallas_call | solution.py:80
  571.1 7.4 %collective-permute-done.32 = bf16[2,192,512]{2,1,0:T(8,128)(2,1)S(1)} collective-permute-done((bf16[2,192,512]{2,1,0:T(8,128)(2,1)S(1)}, bf16[2,192,512]{2,1,0:T(8,128)(2,1)S(1)}, u32[]{:S(2)}, u32[]{:S(2)}) %collective-permute-start.32) | collective-permute-done | bytes 393248 | tf_op jit(solution)/shard_map/ppermute | solution.py:202
  579.7 8.7 %collective-permute-done.33 = bf16[1,192,512]{2,1,0:T(8,128)(2,1)S(1)} collective-permute-done((bf16[1,192,512]{2,1,0:T(8,128)(2,1)S(1)}, bf16[1,192,512]{2,1,0:T(8,128)(2,1)S(1)}, u32[]{:S(2)}, u32[]{:S(2)}) %collective-permute-start.33) | collective-permute-done | bytes 196640 | tf_op jit(solution)/shard_map/ppermute | solution.py:202
  598.1 5.5 collective-permute-done.37
  608.0 16.7 %scatter_rows.3 = bf16[8,2048,512]{2,1,0:T(8,128)(2,1)} custom-call(s32[8,1,256]{2,1,0:T(1,128)} %broadcast_in_dim.14.idx_ref, bf16[8,256,512]{2,1,0:T(8,128)(2,1)} %bitcast.286, bf16[8,2048,512]{2,1,0:T(8,128)(2,1)} %bitcast.273), custom_call_target="tpu_custom_call" | custom-call | tf_op jit(solution)/shard_map/scatter_rows/pallas_call | solution.py:80
  624.6 6.8 %convert_element_type.529 = f32[1024,2048]{1,0:T(8,128)} convert(bf16[1024,2048]{1,0:T(8,128)(2,1)} %all-gather.13.cloned.1.call-done) | non-fusion elementwise | flops 2097152 | bytes 12582912 | tf_op jit(solution)/shard_map/convert_element_type | solution.py:444
  (349 shorter events, 276.4 us)
Async XLA Ops:
  7.2 187.7 %all-gather.7.cloned.1.call-start = ((), (), s32[]{:S(2)}) async-start(), calls=%async_computation | async-start | bytes 4456448 | tf_op jit(solution)/shard_map/all_gather | solution.py:251
  8.3 19.4 %collective-permute-start = (bf16[64,2048]{1,0:T(8,128)(2,1)S(1)}, bf16[64,2048]{1,0:T(8,128)(2,1)S(1)}, u32[]{:S(2)}, u32[]{:S(2)}) collective-permute-start(bf16[64,2048]{1,0:T(8,128)(2,1)S(1)} %constant_dynamic-slice_fusion.15), channel_id=1, source_target_pairs={{0,1},{1,0},{2,3},{3,2},{4,5},{5,4},{6,7},{7,6},{8,9},{9,8},{10,11... | collective-permute-start | bytes 786440 | tf_op jit(solution)/shard_map/ppermute | solution.py:199
  28.4 197.4 %all-gather.9.cloned.1.call-start = ((), (), s32[]{:S(2)}) async-start(), calls=%async_computation.1 | async-start | bytes 4456448 | tf_op jit(solution)/shard_map/all_gather | solution.py:251
  31.5 24.9 %collective-permute-start.2 = (bf16[1024,512]{0,1:T(8,128)(2,1)}, bf16[1024,512]{0,1:T(8,128)(2,1)}, u32[]{:S(2)}, u32[]{:S(2)}) collective-permute-start(bf16[1024,512]{0,1:T(8,128)(2,1)} %bitcast.319), channel_id=1, source_target_pairs={{0,1},{1,0},{2,3},{3,2},{4,5},{5,4},{6,7},{7,6},{8,9},{9,8},{10,11... | collective-permute-start | bytes 3145736 | tf_op jit(solution)/shard_map/ppermute | solution.py:199
  59.6 37.6 %collective-permute-start.3 = (bf16[3,512,512]{2,1,0:T(8,128)(2,1)}, bf16[3,512,512]{2,1,0:T(8,128)(2,1)}, u32[]{:S(2)}, u32[]{:S(2)}) collective-permute-start(bf16[3,512,512]{2,1,0:T(8,128)(2,1)} %constant_dynamic-slice_fusion.11), channel_id=1, source_target_pairs={{0,1},{1,0},{2,3},{3,2},{4,5},{5,4},{6,7},{7,6},{8,9},{9,8},{10,11... | collective-permute-start | bytes 4718600 | tf_op jit(solution)/shard_map/ppermute | solution.py:199
  66.3 522.9 %all-gather.11.cloned.1.call-start = ((), (), s32[]{:S(2)}) async-start(), calls=%async_computation.2 | async-start | bytes 4456448 | tf_op jit(solution)/shard_map/all_gather | solution.py:387
  67.2 56.1 %collective-permute-start.6 = (bf16[256,1024]{1,0:T(8,128)(2,1)}, bf16[256,1024]{1,0:T(8,128)(2,1)}, u32[]{:S(2)}, u32[]{:S(2)}) collective-permute-start(bf16[256,1024]{1,0:T(8,128)(2,1)} %constant_dynamic-slice_fusion.6), channel_id=1, source_target_pairs={{0,1},{1,0},{2,3},{3,2},{4,5},{5,4},{6,7},{7,6},{8,9},{9,8},{10,11... | collective-permute-start | bytes 1572872 | tf_op jit(solution)/shard_map/ppermute | solution.py:199
  97.2 26.6 %collective-permute-start.4 = (bf16[3,512,512]{2,1,0:T(8,128)(2,1)}, bf16[3,512,512]{2,1,0:T(8,128)(2,1)}, u32[]{:S(2)}, u32[]{:S(2)}) collective-permute-start(bf16[3,512,512]{2,1,0:T(8,128)(2,1)} %collective-permute-done.3), channel_id=1, source_target_pairs={{0,2},{2,0},{4,6},{6,4},{8,10},{10,8},{12,14},{14,12},{16,18},{18,... | collective-permute-start | bytes 4718600 | tf_op jit(solution)/shard_map/ppermute | solution.py:202
  123.2 24.3 %collective-permute-start.7 = (bf16[256,1024]{1,0:T(8,128)(2,1)}, bf16[256,1024]{1,0:T(8,128)(2,1)}, u32[]{:S(2)}, u32[]{:S(2)}) collective-permute-start(bf16[256,1024]{1,0:T(8,128)(2,1)} %collective-permute-done.6), channel_id=1, source_target_pairs={{0,2},{2,0},{4,6},{6,4},{8,10},{10,8},{12,14},{14,12},{16,18},{18,... | collective-permute-start | bytes 1572872 | tf_op jit(solution)/shard_map/ppermute | solution.py:202
  158.6 25.4 %collective-permute-start.5 = (bf16[1024,512]{0,1:T(8,128)(2,1)}, bf16[1024,512]{0,1:T(8,128)(2,1)}, u32[]{:S(2)}, u32[]{:S(2)}) collective-permute-start(bf16[1024,512]{0,1:T(8,128)(2,1)} %bitcast.320), channel_id=1, source_target_pairs={{0,1},{1,0},{2,3},{3,2},{4,5},{5,4},{6,7},{7,6},{8,9},{9,8},{10,11... | collective-permute-start | bytes 3145736 | tf_op jit(solution)/shard_map/ppermute | solution.py:199
  214.7 19.9 %collective-permute-start.9 = (bf16[8,128,1024]{2,1,0:T(8,128)(2,1)}, bf16[8,128,1024]{2,1,0:T(8,128)(2,1)}, u32[]{:S(2)}, u32[]{:S(2)}) collective-permute-start(bf16[8,128,1024]{2,1,0:T(8,128)(2,1)} %dynamic-slice_bitcast_fusion.2), channel_id=1, source_target_pairs={{0,2},{2,0},{4,6},{6,4},{8,10},{10,8},{12,14},{14,12},{16,18},{18,... | collective-permute-start | bytes 6291464 | tf_op jit(solution)/shard_map/ppermute | solution.py:202
  219.1 21.0 %collective-permute-start.8 = (bf16[8,128,1024]{2,1,0:T(8,128)(2,1)}, bf16[8,128,1024]{2,1,0:T(8,128)(2,1)}, u32[]{:S(2)}, u32[]{:S(2)}) collective-permute-start(bf16[8,128,1024]{2,1,0:T(8,128)(2,1)} %dynamic-slice_bitcast_fusion.3), channel_id=1, source_target_pairs={{0,2},{2,0},{4,6},{6,4},{8,10},{10,8},{12,14},{14,12},{16,18},{18,... | collective-permute-start | bytes 6291464 | tf_op jit(solution)/shard_map/ppermute | solution.py:202
  244.1 48.3 %collective-permute-start.12 = (bf16[8,128,1024]{2,1,0:T(8,128)(2,1)}, bf16[8,128,1024]{2,1,0:T(8,128)(2,1)}, u32[]{:S(2)}, u32[]{:S(2)}) collective-permute-start(bf16[8,128,1024]{2,1,0:T(8,128)(2,1)} %fusion.40), channel_id=1, source_target_pairs={{0,1},{1,0},{2,3},{3,2},{4,5},{5,4},{6,7},{7,6},{8,9},{9,8},{10,11... | collective-permute-start | bytes 6291464 | tf_op jit(solution)/shard_map/ppermute | solution.py:199
  256.9 23.5 %collective-permute-start.11 = (bf16[8,64,2048]{2,1,0:T(8,128)(2,1)}, bf16[8,64,2048]{2,1,0:T(8,128)(2,1)}, u32[]{:S(2)}, u32[]{:S(2)}) collective-permute-start(bf16[8,64,2048]{2,1,0:T(8,128)(2,1)} %dynamic-slice_bitcast_fusion), channel_id=1, source_target_pairs={{0,2},{2,0},{4,6},{6,4},{8,10},{10,8},{12,14},{14,12},{16,18},{18,... | collective-permute-start | bytes 6291464 | tf_op jit(solution)/shard_map/ppermute | solution.py:202
  259.5 25.5 %collective-permute-start.10 = (bf16[8,64,2048]{2,1,0:T(8,128)(2,1)}, bf16[8,64,2048]{2,1,0:T(8,128)(2,1)}, u32[]{:S(2)}, u32[]{:S(2)}) collective-permute-start(bf16[8,64,2048]{2,1,0:T(8,128)(2,1)} %dynamic-slice_bitcast_fusion.1), channel_id=1, source_target_pairs={{0,2},{2,0},{4,6},{6,4},{8,10},{10,8},{12,14},{14,12},{16,18},{18,... | collective-permute-start | bytes 6291464 | tf_op jit(solution)/shard_map/ppermute | solution.py:202
  295.0 32.4 %collective-permute-start.13 = (bf16[4,128,1024]{2,1,0:T(8,128)(2,1)S(1)}, bf16[4,128,1024]{2,1,0:T(8,128)(2,1)S(1)}, u32[]{:S(2)}, u32[]{:S(2)}) collective-permute-start(bf16[4,128,1024]{2,1,0:T(8,128)(2,1)S(1)} %dynamic-slice_bitcast_fusion.9), channel_id=1, source_target_pairs={{0,4},{2,6},{4,0},{6,2},{8,12},{10,14},{12,8},{14,10},{16,20},{18,... | collective-permute-start | bytes 3145736 | tf_op jit(solution)/shard_map/ppermute | solution.py:202
  318.4 47.2 %collective-permute-start.15 = (bf16[8,64,2048]{2,1,0:T(8,128)(2,1)}, bf16[8,64,2048]{2,1,0:T(8,128)(2,1)}, u32[]{:S(2)}, u32[]{:S(2)}) collective-permute-start(bf16[8,64,2048]{2,1,0:T(8,128)(2,1)} %fusion.38), channel_id=1, source_target_pairs={{0,1},{1,0},{2,3},{3,2},{4,5},{5,4},{6,7},{7,6},{8,9},{9,8},{10,11... | collective-permute-start | bytes 6291464 | tf_op jit(solution)/shard_map/ppermute | solution.py:199
  329.7 20.9 %collective-permute-start.17 = (bf16[8,64,512]{2,1,0:T(8,128)(2,1)}, bf16[8,64,512]{2,1,0:T(8,128)(2,1)}, u32[]{:S(2)}, u32[]{:S(2)}) collective-permute-start(bf16[8,64,512]{2,1,0:T(8,128)(2,1)} %dynamic-slice_bitcast_fusion.12), channel_id=1, source_target_pairs={{0,2},{2,0},{4,6},{6,4},{8,10},{10,8},{12,14},{14,12},{16,18},{18,... | collective-permute-start | bytes 1572872 | tf_op jit(solution)/shard_map/ppermute | solution.py:202
  330.6 22.4 %collective-permute-start.16 = (bf16[8,64,512]{2,1,0:T(8,128)(2,1)}, bf16[8,64,512]{2,1,0:T(8,128)(2,1)}, u32[]{:S(2)}, u32[]{:S(2)}) collective-permute-start(bf16[8,64,512]{2,1,0:T(8,128)(2,1)} %dynamic-slice_bitcast_fusion.13), channel_id=1, source_target_pairs={{0,2},{2,0},{4,6},{6,4},{8,10},{10,8},{12,14},{14,12},{16,18},{18,... | collective-permute-start | bytes 1572872 | tf_op jit(solution)/shard_map/ppermute | solution.py:202
  333.0 22.2 %collective-permute-start.14 = (bf16[2,128,1024]{2,1,0:T(8,128)(2,1)}, bf16[2,128,1024]{2,1,0:T(8,128)(2,1)}, u32[]{:S(2)}, u32[]{:S(2)}) collective-permute-start(bf16[2,128,1024]{2,1,0:T(8,128)(2,1)} %dynamic-slice_bitcast_fusion.14), channel_id=1, source_target_pairs={{0,8},{2,10},{4,12},{6,14},{8,0},{10,2},{12,4},{14,6},{16,24},{18,... | collective-permute-start | bytes 1572872 | tf_op jit(solution)/shard_map/ppermute | solution.py:202
  387.1 33.0 %collective-permute-start.20 = (bf16[8,192,512]{2,1,0:T(8,128)(2,1)}, bf16[8,192,512]{2,1,0:T(8,128)(2,1)}, u32[]{:S(2)}, u32[]{:S(2)}) collective-permute-start(bf16[8,192,512]{2,1,0:T(8,128)(2,1)} %dynamic-slice_bitcast_fusion.5), channel_id=1, source_target_pairs={{0,2},{2,0},{4,6},{6,4},{8,10},{10,8},{12,14},{14,12},{16,18},{18,... | collective-permute-start | bytes 4718600 | tf_op jit(solution)/shard_map/ppermute | solution.py:202
  387.1 202.1 %all-gather.13.cloned.1.call-start = ((), (), s32[]{:S(2)}) async-start(), calls=%async_computation.3 | async-start | bytes 4456448 | tf_op jit(solution)/shard_map/all_gather | solution.py:408
  389.5 28.7 %collective-permute-start.19 = (bf16[4,64,2048]{2,1,0:T(8,128)(2,1)}, bf16[4,64,2048]{2,1,0:T(8,128)(2,1)}, u32[]{:S(2)}, u32[]{:S(2)}) collective-permute-start(bf16[4,64,2048]{2,1,0:T(8,128)(2,1)} %dynamic-slice_bitcast_fusion.8), channel_id=1, source_target_pairs={{0,4},{2,6},{4,0},{6,2},{8,12},{10,14},{12,8},{14,10},{16,20},{18,... | collective-permute-start | bytes 3145736 | tf_op jit(solution)/shard_map/ppermute | solution.py:202
  424.9 21.9 %collective-permute-start.22 = (bf16[2,64,2048]{2,1,0:T(8,128)(2,1)}, bf16[2,64,2048]{2,1,0:T(8,128)(2,1)}, u32[]{:S(2)}, u32[]{:S(2)}) collective-permute-start(bf16[2,64,2048]{2,1,0:T(8,128)(2,1)} %dynamic-slice_bitcast_fusion.11), channel_id=1, source_target_pairs={{0,8},{2,10},{4,12},{6,14},{8,0},{10,2},{12,4},{14,6},{16,24},{18,... | collective-permute-start | bytes 1572872 | tf_op jit(solution)/shard_map/ppermute | solution.py:202
  448.2 18.7 %collective-permute-start.25 = (bf16[2,64,512]{2,1,0:T(8,128)(2,1)S(1)}, bf16[2,64,512]{2,1,0:T(8,128)(2,1)S(1)}, u32[]{:S(2)}, u32[]{:S(2)}) collective-permute-start(bf16[2,64,512]{2,1,0:T(8,128)(2,1)S(1)} %dynamic-slice_bitcast_fusion.17), channel_id=1, source_target_pairs={{0,8},{2,10},{4,12},{6,14},{8,0},{10,2},{12,4},{14,6},{16,24},{18,... | collective-permute-start | bytes 393224 | tf_op jit(solution)/shard_map/ppermute | solution.py:202
  448.9 18.1 %collective-permute-start.24 = (bf16[1,64,2048]{2,1,0:T(8,128)(2,1)S(1)}, bf16[1,64,2048]{2,1,0:T(8,128)(2,1)S(1)}, u32[]{:S(2)}, u32[]{:S(2)}) collective-permute-start(bf16[1,64,2048]{2,1,0:T(8,128)(2,1)S(1)} %constant_dynamic-slice_fusion.4), channel_id=1, source_target_pairs={{0,16},{2,18},{4,20},{6,22},{8,24},{10,26},{12,28},{14,30},{16,0},... | collective-permute-start | bytes 786440 | tf_op jit(solution)/shard_map/ppermute | solution.py:202
  467.8 169.1 %all-gather.15.cloned.1.call-start = ((), (), s32[]{:S(2)}) async-start(), calls=%async_computation.4 | async-start | bytes 4456448 | tf_op jit(solution)/shard_map/all_gather | solution.py:439
  469.1 23.7 %collective-permute-start.28 = (bf16[1024,512]{0,1:T(8,128)(2,1)S(1)}, bf16[1024,512]{0,1:T(8,128)(2,1)S(1)}, u32[]{:S(2)}, u32[]{:S(2)}) collective-permute-start(bf16[1024,512]{0,1:T(8,128)(2,1)S(1)} %dynamic-slice_bitcast_fusion.7), channel_id=1, source_target_pairs={{0,1},{1,0},{2,3},{3,2},{4,5},{5,4},{6,7},{7,6},{8,9},{9,8},{10,11... | collective-permute-start | bytes 3145736 | tf_op jit(solution)/shard_map/ppermute | solution.py:199
  500.2 33.9 %collective-permute-start.27 = (bf16[8,192,512]{2,1,0:T(8,128)(2,1)}, bf16[8,192,512]{2,1,0:T(8,128)(2,1)S(1)}, u32[]{:S(2)}, u32[]{:S(2)}) collective-permute-start(bf16[8,192,512]{2,1,0:T(8,128)(2,1)} %fusion.43), channel_id=1, source_target_pairs={{0,1},{1,0},{2,3},{3,2},{4,5},{5,4},{6,7},{7,6},{8,9},{9,8},{10,11... | collective-permute-start | bytes 4718600 | tf_op jit(solution)/shard_map/ppermute | solution.py:199
  503.1 31.0 %collective-permute-start.26 = (bf16[8,192,512]{2,1,0:T(8,128)(2,1)S(1)}, bf16[8,192,512]{2,1,0:T(8,128)(2,1)S(1)}, u32[]{:S(2)}, u32[]{:S(2)}) collective-permute-start(bf16[8,192,512]{2,1,0:T(8,128)(2,1)S(1)} %dynamic-slice_bitcast_fusion.4), channel_id=1, source_target_pairs={{0,2},{2,0},{4,6},{6,4},{8,10},{10,8},{12,14},{14,12},{16,18},{18,... | collective-permute-start | bytes 4718600 | tf_op jit(solution)/shard_map/ppermute | solution.py:202
  535.8 25.9 %collective-permute-start.29 = (bf16[4,192,512]{2,1,0:T(8,128)(2,1)}, bf16[4,192,512]{2,1,0:T(8,128)(2,1)}, u32[]{:S(2)}, u32[]{:S(2)}) collective-permute-start(bf16[4,192,512]{2,1,0:T(8,128)(2,1)} %dynamic-slice_bitcast_fusion.10), channel_id=1, source_target_pairs={{0,4},{2,6},{4,0},{6,2},{8,12},{10,14},{12,8},{14,10},{16,20},{18,... | collective-permute-start | bytes 2359304 | tf_op jit(solution)/shard_map/ppermute | solution.py:202
  538.5 25.7 %collective-permute-start.30 = (bf16[1024,512]{0,1:T(8,128)(2,1)}, bf16[1024,512]{0,1:T(8,128)(2,1)}, u32[]{:S(2)}, u32[]{:S(2)}) collective-permute-start(bf16[1024,512]{0,1:T(8,128)(2,1)} %dynamic-slice_bitcast_fusion.6), channel_id=1, source_target_pairs={{0,1},{1,0},{2,3},{3,2},{4,5},{5,4},{6,7},{7,6},{8,9},{9,8},{10,11... | collective-permute-start | bytes 3145736 | tf_op jit(solution)/shard_map/ppermute | solution.py:199
  (85 other events, 938.8 us)
Sparse Core Ops, SparseCore 0:
  28.5 52.1 all-gather.6
  82.9 48.9 all-gather.8
  387.2 59.9 all-gather.10
  467.9 49.1 all-gather.12
  589.3 47.5 all-gather.14
